TPU v7x, 512 devices: a whole 4x4x16 slice. The times are simulated.
512 devices in a mesh: dp: 8 (over z_hi, core), ctx: 64 (over x, z_lo, y).
Axes of the slice: x: 4, y: 4, z: 16 (z_hi: 4, z_lo: 4; z = z_hi * 4 + z_lo), core: 2. Of those that a mesh axis runs over, the one named last changes fastest.
Arguments:
- queries: bfloat16 [8, 2048, 8192], P('dp', None, 'ctx'), may hold values from -6 to 6
- keys: bfloat16 [8, 2048, 8192], P('dp', None, 'ctx'), may hold values from -6 to 6
- values: bfloat16 [8, 2048, 8192], P('dp', None, 'ctx'), may hold values from -6 to 6
- cotangent: bfloat16 [8, 2048, 8192], P('dp', None, 'ctx'), may hold values from -6 to 6
- residues: float32 [2048, 16], P(('dp', 'ctx')), may hold values from -1.5 to 1.5
- decays: float32 [2048, 16], P(('dp', 'ctx')), may hold values from 0.1 to 800
Outputs:
- mixed: bfloat16 [8, 2048, 8192], P('dp', None, 'ctx')
- grad_queries: bfloat16 [8, 2048, 8192], P('dp', None, 'ctx')
- grad_keys: bfloat16 [8, 2048, 8192], P('dp', None, 'ctx')
- grad_values: bfloat16 [8, 2048, 8192], P('dp', None, 'ctx')
- grad_residues: float32 [2048, 16], P(('dp', 'ctx'))
All inputs are finite; a program needn't handle non-finite values.
Results may differ from a plain program's by a relative error of at most 0.0057.
Values may be sent and summed in bfloat16 or wider, within the bound.
A program may use at most 64 MiB of HBM per device.

v0:
```python
import functools
import math

import jax
import jax.numpy as jnp
from jax import lax
from jax.experimental import pallas as pl
from jax.sharding import PartitionSpec as P

exact_mode = lax.Precision.HIGHEST


def split_dot(x, tri):
    hi = x.astype(jnp.bfloat16)
    lo = (x - hi.astype(jnp.float32)).astype(jnp.bfloat16)
    return jnp.dot(hi, tri, preferred_element_type=jnp.float32) + jnp.dot(
        lo, tri, preferred_element_type=jnp.float32
    )


def chunk_kernel(k_ref, v_ref, c_ref, q_ref, dec_ref, w_ref, conv_ref, back_ref, stats_ref, *, length):
    f32 = jnp.float32
    rows, chunk = k_ref.shape
    order = dec_ref.shape[1]
    mid = chunk // 2
    g = (k_ref[...].astype(f32) * v_ref[...].astype(f32)).astype(jnp.bfloat16).astype(f32)
    gg = (c_ref[...].astype(f32) * q_ref[...].astype(f32)).astype(jnp.bfloat16).astype(f32)
    dec = dec_ref[...]
    w = w_ref[...]
    pos = lax.broadcasted_iota(jnp.int32, (1, chunk), 1).astype(f32)
    row_at = lax.broadcasted_iota(jnp.int32, (chunk, chunk), 0)
    col_at = lax.broadcasted_iota(jnp.int32, (chunk, chunk), 1)
    upper = (row_at <= col_at).astype(jnp.bfloat16)
    lower = (row_at >= col_at).astype(jnp.bfloat16)
    offset = (pos - mid) / length
    conv = jnp.zeros((rows, chunk), f32)
    back = jnp.zeros((rows, chunk), f32)
    for n in range(order):
        a = dec[:, n : n + 1]
        grow = jnp.exp(a * offset)
        shrink = jnp.exp(-a * offset)
        fwd = shrink * split_dot(g * grow, upper)
        bwd = grow * split_dot(gg * shrink, lower)
        conv = conv + w[:, n : n + 1] * fwd
        back = back + w[:, n : n + 1] * bwd
        stats_ref[:, n : n + 1] = fwd[:, chunk - 1 :]
        stats_ref[:, order + n : order + n + 1] = bwd[:, :1]
        stats_ref[:, 2 * order + n : 2 * order + n + 1] = jnp.sum(gg * fwd, axis=1, keepdims=True)
        stats_ref[:, 3 * order + n : 3 * order + n + 1] = jnp.sum(
            gg * shrink, axis=1, keepdims=True
        ) * jnp.exp(-a * ((mid + 1) / length))
    conv_ref[...] = conv
    back_ref[...] = back


def chunk_pass(keys, values, cotangent, queries, dec, weight, length, rows=256):
    channels, chunk = keys.shape
    order = dec.shape[1]
    rows = min(rows, channels)
    wide = pl.BlockSpec((rows, chunk), lambda i: (i, 0))
    narrow = pl.BlockSpec((rows, order), lambda i: (i, 0))
    return pl.pallas_call(
        functools.partial(chunk_kernel, length=length),
        grid=(channels // rows,),
        in_specs=[wide, wide, wide, wide, narrow, narrow],
        out_specs=[wide, wide, pl.BlockSpec((rows, 4 * order), lambda i: (i, 0))],
        out_shape=[
            jax.ShapeDtypeStruct((channels, chunk), jnp.float32),
            jax.ShapeDtypeStruct((channels, chunk), jnp.float32),
            jax.ShapeDtypeStruct((channels, 4 * order), jnp.float32),
        ],
    )(keys, values, cotangent, queries, dec, weight)


def body(queries, keys, values, cotangent, residues, decays):
    n_dp = lax.axis_size("dp")
    n_ctx = lax.axis_size("ctx")
    ctx_at = lax.axis_index("ctx")
    seq_count, channels, chunk = keys.shape
    block, order = residues.shape
    length = chunk * n_ctx
    f32 = jnp.float32

    own = jnp.concatenate([residues, decays], axis=1)
    part = lax.all_to_all(
        jnp.broadcast_to(own[None], (n_dp,) + own.shape), "dp", 0, 0, tiled=True
    ).reshape(n_dp, 1, block, 2 * order)
    params = lax.all_to_all(
        jnp.broadcast_to(part, (n_dp, n_ctx, block, 2 * order)), "ctx", 1, 1, tiled=True
    ).reshape(channels, 2 * order)
    dec = params[:, order:]
    scale = jnp.sqrt(1.0 - jnp.exp(-2.0 * dec / length))
    weight = params[:, :order] * scale

    pos = jnp.arange(chunk, dtype=f32)
    dk = dec[:, :, None]
    conv_intra, back_intra, stats = chunk_pass(
        keys[0], values[0], cotangent[0], queries[0], dec, weight, length
    )
    lead_fwd = jnp.exp(-dk * ((pos + 1) / length))
    lead_bwd = jnp.exp(-dk * ((chunk - pos) / length))

    groups = channels // (n_dp * n_ctx)
    stats = stats.reshape(n_dp, n_ctx, groups, 4 * order)
    stats = lax.all_to_all(stats, "ctx", 1, 1, tiled=True)
    s_fwd = stats[..., :order]
    s_bwd = stats[..., order : 2 * order]
    c_intra = stats[..., 2 * order : 3 * order]
    c_lead = stats[..., 3 * order :]
    dec_grp = lax.dynamic_slice_in_dim(
        dec.reshape(n_dp, n_ctx, groups, order), ctx_at, 1, axis=1
    )
    hop_decay = dec_grp * (chunk / length)

    def exclusive_scan(state, sign):
        pad = jnp.zeros_like(state[:, :1])
        if sign > 0:
            carry = jnp.concatenate([pad, state[:, :-1]], axis=1)
        else:
            carry = jnp.concatenate([state[:, 1:], pad], axis=1)
        hop = 1
        while hop < n_ctx:
            fill = jnp.zeros_like(carry[:, :hop])
            if sign > 0:
                moved = jnp.concatenate([fill, carry[:, :-hop]], axis=1)
            else:
                moved = jnp.concatenate([carry[:, hop:], fill], axis=1)
            carry = carry + jnp.exp(-hop_decay * hop) * moved
            hop *= 2
        return carry

    carry_fwd = exclusive_scan(s_fwd, 1)
    carry_bwd = exclusive_scan(s_bwd, -1)
    cross_grp = jnp.sum(c_intra + carry_fwd * c_lead, axis=1)
    carries = lax.all_to_all(
        jnp.concatenate([carry_fwd, carry_bwd], axis=-1), "ctx", 1, 1, tiled=True
    ).reshape(channels, 2 * order)
    carry_fwd = carries[:, :order]
    carry_bwd = carries[:, order:]
    total = jnp.sum(lax.all_to_all(cross_grp, "dp", 0, 0, tiled=True), axis=0)

    own_scale = jnp.sqrt(1.0 - jnp.exp(-2.0 * decays / length))
    grad_residues = total * own_scale / math.sqrt(seq_count * n_dp * length)

    conv_full = conv_intra + jnp.sum((weight * carry_fwd)[:, :, None] * lead_fwd, axis=1)
    back_full = back_intra + jnp.sum((weight * carry_bwd)[:, :, None] * lead_bwd, axis=1)
    conv_f = conv_full.astype(jnp.bfloat16).astype(f32)[None]
    back_f = back_full.astype(jnp.bfloat16).astype(f32)[None]
    mixed = (queries.astype(f32) * conv_f).astype(jnp.bfloat16)
    grad_queries = (cotangent.astype(f32) * conv_f).astype(jnp.bfloat16)
    grad_keys = (back_f * values.astype(f32)).astype(jnp.bfloat16)
    grad_values = (back_f * keys.astype(f32)).astype(jnp.bfloat16)
    return (mixed, grad_queries, grad_keys, grad_values, grad_residues)


def solution(mesh):
    return jax.shard_map(
        body,
        mesh=mesh,
        in_specs=(
            P("dp", None, "ctx"),
            P("dp", None, "ctx"),
            P("dp", None, "ctx"),
            P("dp", None, "ctx"),
            P(("dp", "ctx"), None),
            P(("dp", "ctx"), None),
        ),
        out_specs=(
            P("dp", None, "ctx"),
            P("dp", None, "ctx"),
            P("dp", None, "ctx"),
            P("dp", None, "ctx"),
            P(("dp", "ctx"), None),
        ),
        check_vma=False,
    )
```

profile of v0, /device:TPU:1, one launch (start us, length us, event | category | flops | bytes accessed | tf_op | source)
XLA Modules:
  0.0 217.6 jit_solution(6647488216922945481)
XLA Ops:
  0.6 0.8 pad_maximum_fusion.1
  1.5 28.2 %all_to_all.25 = f32[8,1,128]{2,1,0:T(1,128)S(1)} all-to-all(f32[8,1,128]{2,1,0:T(1,128)S(1)} %reshape.45), channel_id=1, replica_groups=mesh['dp'=8,'ctx'=64] {'dp'}, dimensions={0} | all-to-all | bytes 8192 | tf_op jit(solution)/shard_map/all_to_all | solution.py:85
  31.2 0.7 reshape.47
  31.9 19.7 %all_to_all.26 = f32[64,1,1024]{2,1,0:T(1,128)S(1)} all-to-all(f32[64,1,1024]{2,1,0:T(1,128)S(1)} %reshape.47), channel_id=1, replica_groups=mesh['dp'=8,'ctx'=64] {'ctx'}, dimensions={0} | all-to-all | bytes 524288 | tf_op jit(solution)/shard_map/all_to_all | solution.py:88
  51.5 1.3 reduce.1
  53.5 2.1 slice_negate_fusion
  55.7 69.0 %shard_map.101 = (f32[2048,128]{1,0:T(8,128)}, f32[2048,128]{1,0:T(8,128)}, f32[2048,64]{1,0:T(8,128)}) custom-call(bf16[2048,128]{1,0:T(8,128)(2,1)} %bitcast.47, bf16[2048,128]{1,0:T(8,128)(2,1)} %bitcast.49, bf16[2048,128]{1,0:T(8,128)(2,1)} %bitcast.46, bf16[2048,128]{1,0:T(8,128)(2,1)} %bitcast.48, f32[2048,16]{1,0:T(8,128)} %get-tuple-element.23.dec_ref, ...), custom_call_target="tpu_custom_call" | custom-call | tf_op jit(solution)/shard_map/pallas_call | solution.py:62
  124.7 1.5 copy.23
  126.2 1.8 reshape.49
  128.0 6.3 %all-to-all-start.2 = ((f32[64,1,2048]{2,1,0:T(1,128)}), f32[64,1,2048]{2,1,0:T(1,128)S(1)}, u32[]{:S(2)}, u32[]{:S(2)}) async-start(f32[64,1,2048]{2,1,0:T(1,128)} %reshape.49), calls=%async_computation.2 | async-start | bytes 1048576 | tf_op jit(solution)/shard_map/all_to_all | solution.py:105
  134.3 0.8 exponential_bitcast_fusion
  135.0 16.2 %all-to-all-done.2 = f32[64,1,2048]{2,1,0:T(1,128)S(1)} async-done(((f32[64,1,2048]{2,1,0:T(1,128)}), f32[64,1,2048]{2,1,0:T(1,128)S(1)}, u32[]{:S(2)}, u32[]{:S(2)}) %all-to-all-start.2) | async-done | bytes 524320 | tf_op jit(solution)/shard_map/all_to_all | solution.py:105
  151.2 1.9 reduce.2
  153.1 0.7 reshape.50
  155.0 1.0 multiply_add_fusion.11
  156.2 1.0 multiply_add_fusion.10
  157.4 1.0 multiply_add_fusion.9
  158.5 1.1 multiply_add_fusion.8
  159.8 0.9 multiply_add_fusion.7
  160.8 1.8 fusion.5
  162.6 5.5 %all-to-all-start.4 = ((f32[8,4,16]{2,1,0:T(4,128)}), f32[8,4,16]{2,1,0:T(4,128)S(1)}, u32[]{:S(2)}, u32[]{:S(2)}) async-start(f32[8,4,16]{2,1,0:T(4,128)} %get-tuple-element.13), calls=%async_computation.4 | async-start | bytes 32768 | tf_op jit(solution)/shard_map/all_to_all | solution.py:140
  168.7 1.4 reshape.51
  170.1 9.9 %all-to-all-done.4 = f32[8,4,16]{2,1,0:T(4,128)S(1)} async-done(((f32[8,4,16]{2,1,0:T(4,128)}), f32[8,4,16]{2,1,0:T(4,128)S(1)}, u32[]{:S(2)}, u32[]{:S(2)}) %all-to-all-start.4) | async-done | bytes 2080 | tf_op jit(solution)/shard_map/all_to_all | solution.py:140
  180.0 4.7 %all-to-all-start.3 = ((f32[64,1,1024]{2,1,0:T(1,128)}), f32[64,1,1024]{2,1,0:T(1,128)S(1)}, u32[]{:S(2)}, u32[]{:S(2)}) async-start(f32[64,1,1024]{2,1,0:T(1,128)} %reshape.51), calls=%async_computation.3 | async-start | bytes 524288 | tf_op jit(solution)/shard_map/all_to_all | solution.py:135
  185.3 10.2 %all-to-all-done.3 = f32[64,1,1024]{2,1,0:T(1,128)S(1)} async-done(((f32[64,1,1024]{2,1,0:T(1,128)}), f32[64,1,1024]{2,1,0:T(1,128)S(1)}, u32[]{:S(2)}, u32[]{:S(2)}) %all-to-all-start.3) | async-done | bytes 262176 | tf_op jit(solution)/shard_map/all_to_all | solution.py:135
  195.5 1.3 reduce.3
  197.5 1.0 copy-done
  198.9 0.9 copy-done.7
  199.8 14.5 %multiply_reduce_fusion = (f32[2048,128]{1,0:T(8,128)S(1)}, f32[2048,128]{1,0:T(8,128)S(1)}) fusion(f32[128]{0:T(128)S(1)} %subtract_multiply_fusion, f32[2048,16]{1,0:T(8,128)S(1)} %get-tuple-element.20, f32[2048,16]{1,0:T(8,128)S(1)} %copy-done.7, f32[128]{0:T(128)S(1)} %add_multiply_fusion, f32[2048,16]{1,0:T(8,128)S(1)} %get-tuple-element.19), kind=kLoop, calls=%fused_computation | loop fusion | flops 24641536 | bytes 2491392 | tf_op jit(solution)/shard_map/reduce_sum | solution.py:146
  214.3 1.3 fusion.1
  215.7 0.9 fusion
  216.7 0.9 fusion.2
  (45 shorter events, 6.5 us)
Async XLA Ops:
  128.0 23.3 %all-to-all-start.2 = ((f32[64,1,2048]{2,1,0:T(1,128)}), f32[64,1,2048]{2,1,0:T(1,128)S(1)}, u32[]{:S(2)}, u32[]{:S(2)}) async-start(f32[64,1,2048]{2,1,0:T(1,128)} %reshape.49), calls=%async_computation.2 | async-start | bytes 1048576 | tf_op jit(solution)/shard_map/all_to_all | solution.py:105
  162.6 17.4 %all-to-all-start.4 = ((f32[8,4,16]{2,1,0:T(4,128)}), f32[8,4,16]{2,1,0:T(4,128)S(1)}, u32[]{:S(2)}, u32[]{:S(2)}) async-start(f32[8,4,16]{2,1,0:T(4,128)} %get-tuple-element.13), calls=%async_computation.4 | async-start | bytes 32768 | tf_op jit(solution)/shard_map/all_to_all | solution.py:140
  168.7 16.0 %copy-start.8 = (f32[4,16]{1,0:T(4,128)S(1)}, f32[4,16]{1,0:T(4,128)}, u32[]{:S(2)}) copy-start(f32[4,16]{1,0:T(4,128)} %param.11) | copy-start | bytes 772
  180.0 15.5 %all-to-all-start.3 = ((f32[64,1,1024]{2,1,0:T(1,128)}), f32[64,1,1024]{2,1,0:T(1,128)S(1)}, u32[]{:S(2)}, u32[]{:S(2)}) async-start(f32[64,1,1024]{2,1,0:T(1,128)} %reshape.51), calls=%async_computation.3 | async-start | bytes 524288 | tf_op jit(solution)/shard_map/all_to_all | solution.py:135
  197.3 1.2 copy-start
  198.5 1.2 copy-start.7
  199.8 14.5 %copy-start.1 = (bf16[1,2048,128]{2,1,0:T(8,128)(2,1)S(1)}, bf16[1,2048,128]{2,1,0:T(8,128)(2,1)}, u32[]{:S(2)}) copy-start(bf16[1,2048,128]{2,1,0:T(8,128)(2,1)} %param.9) | copy-start | bytes 1572868
  199.8 14.5 %copy-start.2 = (bf16[1,2048,128]{2,1,0:T(8,128)(2,1)S(1)}, bf16[1,2048,128]{2,1,0:T(8,128)(2,1)}, u32[]{:S(2)}) copy-start(bf16[1,2048,128]{2,1,0:T(8,128)(2,1)} %param.7) | copy-start | bytes 1572868
  199.8 14.6 %copy-start.5 = (f32[2048,128]{1,0:T(8,128)S(1)}, f32[2048,128]{1,0:T(8,128)}, u32[]{:S(2)}) copy-start(f32[2048,128]{1,0:T(8,128)} %get-tuple-element.8) | copy-start | bytes 3145732
  199.8 14.6 %copy-start.6 = (f32[2048,128]{1,0:T(8,128)S(1)}, f32[2048,128]{1,0:T(8,128)}, u32[]{:S(2)}) copy-start(f32[2048,128]{1,0:T(8,128)} %get-tuple-element.10) | copy-start | bytes 3145732
  214.3 1.3 copy-start.3
  215.7 1.0 copy-start.4
where the time goes:
time: 219 us; the launch traced here: 218 us
  Pallas kernels  69 us (32%)
  blocking collectives  47.9 us (22%)
  waiting for transfers between devices  36.3 us (17%)
  other arithmetic  34.9 us (16%)
  starting transfers between devices  16.4 us (7%)
  local copies, waits for them, and re-layouts  12.1 us (6%)
    pallas_call x1, Pallas kernels, chunk_pass(): pl.pallas_call(functools.partial(chunk_kernel, length=length), grid=(chan...  69 us
    all_to_all x1, blocking collectives, body(): lax.all_to_all(jnp.broadcast_to(own[None], (n_dp,) + own.shape), 'dp', 0,...  28.2 us
    all_to_all x1, blocking collectives, body(): lax.all_to_all(jnp.broadcast_to(part, (n_dp, n_ctx, block, 2 * order)), '...  19.7 us
    all_to_all x1, waiting for transfers between devices, body(): stats = lax.all_to_all(stats, 'ctx', 1, 1, tiled=True)  16.2 us
    reduce_sum x1, other arithmetic, body(): jnp.sum((weight * carry_bwd)[:, :, None] * lead_bwd, axis=1)  14.5 us
    all_to_all x1, waiting for transfers between devices, body(): lax.all_to_all(jnp.concatenate([carry_fwd, carry_bwd], axis=-1), 'ctx', 1...  10.2 us
    all_to_all x1, waiting for transfers between devices, body(): total = jnp.sum(lax.all_to_all(cross_grp, 'dp', 0, 0, tiled=True), axis=0)  9.9 us
    unnamed x27, local copies, waits for them, and re-layouts  8.01 us
  transfers between devices with their start and end apart: 3, of which 3 were waited for; matrix products, arithmetic and copies ran while one was open for 2% of the time, Pallas kernels for 0%

commit v1 on v0

--- a/solution.py
+++ b/solution.py
@@ -82,11 +82,9 @@
     f32 = jnp.float32
 
     own = jnp.concatenate([residues, decays], axis=1)
-    part = lax.all_to_all(
-        jnp.broadcast_to(own[None], (n_dp,) + own.shape), "dp", 0, 0, tiled=True
-    ).reshape(n_dp, 1, block, 2 * order)
+    spots = n_dp * n_ctx
     params = lax.all_to_all(
-        jnp.broadcast_to(part, (n_dp, n_ctx, block, 2 * order)), "ctx", 1, 1, tiled=True
+        jnp.broadcast_to(own[None], (spots,) + own.shape), ("dp", "ctx"), 0, 0, tiled=True
     ).reshape(channels, 2 * order)
     dec = params[:, order:]
     scale = jnp.sqrt(1.0 - jnp.exp(-2.0 * dec / length))
@@ -100,16 +98,14 @@
     lead_fwd = jnp.exp(-dk * ((pos + 1) / length))
     lead_bwd = jnp.exp(-dk * ((chunk - pos) / length))
 
-    groups = channels // (n_dp * n_ctx)
-    stats = stats.reshape(n_dp, n_ctx, groups, 4 * order)
-    stats = lax.all_to_all(stats, "ctx", 1, 1, tiled=True)
+    stats = lax.all_to_all(
+        stats.reshape(spots, block, 4 * order), ("dp", "ctx"), 0, 0, tiled=True
+    ).reshape(n_dp, n_ctx, block, 4 * order)
     s_fwd = stats[..., :order]
     s_bwd = stats[..., order : 2 * order]
     c_intra = stats[..., 2 * order : 3 * order]
     c_lead = stats[..., 3 * order :]
-    dec_grp = lax.dynamic_slice_in_dim(
-        dec.reshape(n_dp, n_ctx, groups, order), ctx_at, 1, axis=1
-    )
+    dec_grp = decays[None, None]
     hop_decay = dec_grp * (chunk / length)
 
     def exclusive_scan(state, sign):
@@ -131,13 +127,16 @@
 
     carry_fwd = exclusive_scan(s_fwd, 1)
     carry_bwd = exclusive_scan(s_bwd, -1)
-    cross_grp = jnp.sum(c_intra + carry_fwd * c_lead, axis=1)
+    total = jnp.sum(c_intra + carry_fwd * c_lead, axis=(0, 1))
     carries = lax.all_to_all(
-        jnp.concatenate([carry_fwd, carry_bwd], axis=-1), "ctx", 1, 1, tiled=True
+        jnp.concatenate([carry_fwd, carry_bwd], axis=-1).reshape(spots, block, 2 * order),
+        ("dp", "ctx"),
+        0,
+        0,
+        tiled=True,
     ).reshape(channels, 2 * order)
     carry_fwd = carries[:, :order]
     carry_bwd = carries[:, order:]
-    total = jnp.sum(lax.all_to_all(cross_grp, "dp", 0, 0, tiled=True), axis=0)
 
     own_scale = jnp.sqrt(1.0 - jnp.exp(-2.0 * decays / length))
     grad_residues = total * own_scale / math.sqrt(seq_count * n_dp * length)

time: 219 us -> 236 us (1.078)
  waiting for transfers between devices: 36.3 us -> 59.7 us
  other arithmetic: 34.9 us -> 31 us
  local copies, waits for them, and re-layouts: 12.1 us -> 8.78 us
    all_to_all x3 -> x2, waiting for transfers between devices: 36.3 us -> 59.7 us  [the longest x1 35.8 us: body(): lax.all_to_all(stats.reshape(spots, block, 4 * order), ('dp', 'ctx'), 0,...]
    all_to_all x3 -> x2, starting transfers between devices: 16.4 us -> 18 us  [the longest x1 9.13 us: body(): lax.all_to_all(stats.reshape(spots, block, 4 * order), ('dp', 'ctx'), 0,...]
    unnamed x27 -> x22, local copies, waits for them, and re-layouts: 8.01 us -> 6.5 us
    all_to_all x2 -> x1, blocking collectives: 47.9 us -> 48.6 us  [body(): lax.all_to_all(jnp.broadcast_to(own[None], (spots,) + own.shape), ('dp',...]
    all_to_all x4 -> x3, other arithmetic: 5.06 us -> 4.4 us  [the longest x1 1.88 us: body(): lax.all_to_all(stats.reshape(spots, block, 4 * order), ('dp', 'ctx'), 0,...]
  transfers between devices with their start and end apart: 3 -> 2, of which waited for: 3 -> 2; matrix products, arithmetic and copies ran while one was open for 2% -> 0% of each run, Pallas kernels for 0% -> 0%
where the time goes in v1:
time: 236 us
  Pallas kernels  69 us (29%)
  waiting for transfers between devices  59.7 us (25%)
  blocking collectives  48.6 us (21%)
  other arithmetic  31 us (13%)
  starting transfers between devices  18 us (8%)
  local copies, waits for them, and re-layouts  8.78 us (4%)
    pallas_call x1, Pallas kernels, chunk_pass(): pl.pallas_call(functools.partial(chunk_kernel, length=length), grid=(chan...  69 us
    all_to_all x1, blocking collectives, body(): lax.all_to_all(jnp.broadcast_to(own[None], (spots,) + own.shape), ('dp',...  48.6 us
    all_to_all x1, waiting for transfers between devices, body(): lax.all_to_all(stats.reshape(spots, block, 4 * order), ('dp', 'ctx'), 0,...  35.8 us
    all_to_all x1, waiting for transfers between devices, body(): lax.all_to_all(jnp.concatenate([carry_fwd, carry_bwd], axis=-1).reshape(s...  23.9 us
    reduce_sum x1, other arithmetic, body(): jnp.sum((weight * carry_bwd)[:, :, None] * lead_bwd, axis=1)  14.5 us
    all_to_all x1, starting transfers between devices, body(): lax.all_to_all(stats.reshape(spots, block, 4 * order), ('dp', 'ctx'), 0,...  9.13 us
    all_to_all x1, starting transfers between devices, body(): lax.all_to_all(jnp.concatenate([carry_fwd, carry_bwd], axis=-1).reshape(s...  8.86 us
    unnamed x22, local copies, waits for them, and re-layouts  6.5 us
  transfers between devices with their start and end apart: 2, of which 2 were waited for; matrix products, arithmetic and copies ran while one was open for 0% of the time, Pallas kernels for 0%

profile of v1, /device:TPU:1, one launch (start us, length us, event | category | flops | bytes accessed | tf_op | source)
XLA Modules:
  0.0 236.1 jit_solution(12629397249328480546)
XLA Ops:
  0.6 0.8 pad_maximum_fusion.1
  1.5 0.7 reshape.66
  2.2 48.6 %all_to_all.15 = f32[512,1,128]{2,1,0:T(1,128)S(1)} all-to-all(f32[512,1,128]{2,1,0:T(1,128)S(1)} %reshape.66), channel_id=1, replica_groups=mesh['dp'=8,'ctx'=64] {'dp','ctx'}, dimensions={0} | all-to-all | bytes 524288 | tf_op jit(solution)/shard_map/all_to_all | solution.py:86
  50.8 0.5 broadcast.104
  51.3 1.3 reduce
  52.6 0.4 reshape.67
  53.0 1.8 slice_negate_fusion
  54.8 69.0 %shard_map.101 = (f32[2048,128]{1,0:T(8,128)}, f32[2048,128]{1,0:T(8,128)}, f32[2048,64]{1,0:T(8,128)}) custom-call(bf16[2048,128]{1,0:T(8,128)(2,1)} %bitcast.23, bf16[2048,128]{1,0:T(8,128)(2,1)} %bitcast.25, bf16[2048,128]{1,0:T(8,128)(2,1)} %bitcast.22, bf16[2048,128]{1,0:T(8,128)(2,1)} %bitcast.24, f32[2048,16]{1,0:T(8,128)} %get-tuple-element.23.dec_ref, ...), custom_call_target="tpu_custom_call" | custom-call | tf_op jit(solution)/shard_map/pallas_call | solution.py:62
  123.8 3.0 %reshape.68 = f32[512,1,256]{2,1,0:T(1,128)} reshape(f32[512,4,64]{2,1,0:T(4,128)} %bitcast.26) | data formatting | bytes 1048576
  126.8 9.1 %all-to-all-start.1 = ((f32[512,1,256]{2,1,0:T(1,128)}), f32[512,1,256]{2,1,0:T(1,128)S(1)}, u32[]{:S(2)}, u32[]{:S(2)}) async-start(f32[512,1,256]{2,1,0:T(1,128)} %reshape.68), calls=%async_computation.1 | async-start | bytes 1048576 | tf_op jit(solution)/shard_map/all_to_all | solution.py:101
  136.0 35.8 %all-to-all-done.1 = f32[512,1,256]{2,1,0:T(1,128)S(1)} async-done(((f32[512,1,256]{2,1,0:T(1,128)}), f32[512,1,256]{2,1,0:T(1,128)S(1)}, u32[]{:S(2)}, u32[]{:S(2)}) %all-to-all-start.1) | async-done | bytes 524320 | tf_op jit(solution)/shard_map/all_to_all | solution.py:101
  171.8 1.9 reduce.1
  173.7 0.5 reshape.69
  174.2 0.6 fusion.11
  175.3 0.7 multiply_add_fusion.11
  176.1 0.7 multiply_add_fusion.10
  177.0 0.7 multiply_add_fusion.9
  177.9 0.6 multiply_add_fusion.8
  178.6 0.6 multiply_add_fusion.7
  179.3 1.3 fusion.5
  180.7 0.6 pad_maximum_fusion
  181.3 1.4 reshape.70
  182.7 8.9 %all-to-all-start.2 = ((f32[512,1,128]{2,1,0:T(1,128)}), f32[512,1,128]{2,1,0:T(1,128)S(1)}, u32[]{:S(2)}, u32[]{:S(2)}) async-start(f32[512,1,128]{2,1,0:T(1,128)} %reshape.70), calls=%async_computation.2 | async-start | bytes 524288 | tf_op jit(solution)/shard_map/all_to_all | solution.py:131
  191.6 0.6 multiply_multiply_fusion
  192.2 23.9 %all-to-all-done.2 = f32[512,1,128]{2,1,0:T(1,128)S(1)} async-done(((f32[512,1,128]{2,1,0:T(1,128)}), f32[512,1,128]{2,1,0:T(1,128)S(1)}, u32[]{:S(2)}, u32[]{:S(2)}) %all-to-all-start.2) | async-done | bytes 262176 | tf_op jit(solution)/shard_map/all_to_all | solution.py:131
  216.1 1.3 reduce.2
  217.3 0.4 reshape.71
  217.8 0.3 slice_multiply_fusion.2
  218.2 14.5 %multiply_reduce_fusion = (f32[2048,128]{1,0:T(8,128)S(1)}, f32[2048,128]{1,0:T(8,128)S(1)}) fusion(f32[128]{0:T(128)S(1)} %subtract_multiply_fusion, f32[2048,16]{1,0:T(8,128)S(1)} %get-tuple-element.20, f32[2048,16]{1,0:T(8,128)S(1)} %get-tuple-element.21, f32[128]{0:T(128)S(1)} %add_multiply_fusion, f32[2048,16]{1,0:T(8,128)S(1)} %get-tuple-element.19), kind=kLoop, calls=%fused_computation | loop fusion | flops 24641536 | bytes 2491392 | tf_op jit(solution)/shard_map/reduce_sum | solution.py:145
  232.8 1.3 fusion.1
  234.1 0.9 fusion
  235.1 0.9 fusion.2
  (32 shorter events, 1.3 us)
Async XLA Ops:
  123.8 12.1 %copy-start.7 = (f32[4,16]{1,0:T(4,128)S(1)}, f32[4,16]{1,0:T(4,128)}, u32[]{:S(2)}) copy-start(f32[4,16]{1,0:T(4,128)} %param.11) | copy-start | bytes 772
  126.8 45.0 %all-to-all-start.1 = ((f32[512,1,256]{2,1,0:T(1,128)}), f32[512,1,256]{2,1,0:T(1,128)S(1)}, u32[]{:S(2)}, u32[]{:S(2)}) async-start(f32[512,1,256]{2,1,0:T(1,128)} %reshape.68), calls=%async_computation.1 | async-start | bytes 1048576 | tf_op jit(solution)/shard_map/all_to_all | solution.py:101
  182.7 33.4 %all-to-all-start.2 = ((f32[512,1,128]{2,1,0:T(1,128)}), f32[512,1,128]{2,1,0:T(1,128)S(1)}, u32[]{:S(2)}, u32[]{:S(2)}) async-start(f32[512,1,128]{2,1,0:T(1,128)} %reshape.70), calls=%async_computation.2 | async-start | bytes 524288 | tf_op jit(solution)/shard_map/all_to_all | solution.py:131
  191.5 26.3 %copy-start = (f32[2048,16]{1,0:T(8,128)S(1)}, f32[2048,16]{1,0:T(8,128)}, u32[]{:S(2)}) copy-start(f32[2048,16]{1,0:T(8,128)} %get-tuple-element.22.w_ref) | copy-start | bytes 393220
  218.1 14.6 %copy-start.1 = (bf16[1,2048,128]{2,1,0:T(8,128)(2,1)S(1)}, bf16[1,2048,128]{2,1,0:T(8,128)(2,1)}, u32[]{:S(2)}) copy-start(bf16[1,2048,128]{2,1,0:T(8,128)(2,1)} %param.9) | copy-start | bytes 1572868
  218.2 14.6 %copy-start.2 = (bf16[1,2048,128]{2,1,0:T(8,128)(2,1)S(1)}, bf16[1,2048,128]{2,1,0:T(8,128)(2,1)}, u32[]{:S(2)}) copy-start(bf16[1,2048,128]{2,1,0:T(8,128)(2,1)} %param.7) | copy-start | bytes 1572868
  218.2 14.6 %copy-start.5 = (f32[2048,128]{1,0:T(8,128)S(1)}, f32[2048,128]{1,0:T(8,128)}, u32[]{:S(2)}) copy-start(f32[2048,128]{1,0:T(8,128)} %get-tuple-element.8) | copy-start | bytes 3145732
  218.2 14.6 %copy-start.6 = (f32[2048,128]{1,0:T(8,128)S(1)}, f32[2048,128]{1,0:T(8,128)}, u32[]{:S(2)}) copy-start(f32[2048,128]{1,0:T(8,128)} %get-tuple-element.10) | copy-start | bytes 3145732
  232.8 1.3 copy-start.3
  234.1 1.0 copy-start.4

commit v2 on v0

--- a/solution.py
+++ b/solution.py
@@ -33,6 +33,16 @@
     upper = (row_at <= col_at).astype(jnp.bfloat16)
     lower = (row_at >= col_at).astype(jnp.bfloat16)
     offset = (pos - mid) / length
+    lane_at = lax.broadcasted_iota(jnp.int32, (8, 4 * chunk), 1)
+    kind_at = lax.broadcasted_iota(jnp.int32, (8, 4 * chunk), 0)
+    part_at = lane_at // chunk
+    pick = (
+        ((kind_at == 0) & (lane_at == chunk - 1))
+        | ((kind_at == 1) & (lane_at == chunk))
+        | ((kind_at == 2) & (part_at == 2))
+        | ((kind_at == 3) & (part_at == 3))
+    ).astype(jnp.bfloat16)
+    rows_by_lanes = (((1,), (1,)), ((), ()))
     conv = jnp.zeros((rows, chunk), f32)
     back = jnp.zeros((rows, chunk), f32)
     for n in range(order):
@@ -43,12 +53,14 @@
         bwd = grow * split_dot(gg * shrink, lower)
         conv = conv + w[:, n : n + 1] * fwd
         back = back + w[:, n : n + 1] * bwd
-        stats_ref[:, n : n + 1] = fwd[:, chunk - 1 :]
-        stats_ref[:, order + n : order + n + 1] = bwd[:, :1]
-        stats_ref[:, 2 * order + n : 2 * order + n + 1] = jnp.sum(gg * fwd, axis=1, keepdims=True)
-        stats_ref[:, 3 * order + n : 3 * order + n + 1] = jnp.sum(
-            gg * shrink, axis=1, keepdims=True
-        ) * jnp.exp(-a * ((mid + 1) / length))
+        lead = shrink * jnp.exp(-a * ((mid + 1) / length))
+        joined = jnp.concatenate([fwd, bwd, gg * fwd, gg * lead], axis=1)
+        hi = joined.astype(jnp.bfloat16)
+        lo = (joined - hi.astype(f32)).astype(jnp.bfloat16)
+        picked = lax.dot_general(
+            pick, hi, rows_by_lanes, preferred_element_type=f32
+        ) + lax.dot_general(pick, lo, rows_by_lanes, preferred_element_type=f32)
+        stats_ref[4 * n : 4 * n + 4, :] = picked[:4]
     conv_ref[...] = conv
     back_ref[...] = back
 
@@ -63,11 +75,11 @@
         functools.partial(chunk_kernel, length=length),
         grid=(channels // rows,),
         in_specs=[wide, wide, wide, wide, narrow, narrow],
-        out_specs=[wide, wide, pl.BlockSpec((rows, 4 * order), lambda i: (i, 0))],
+        out_specs=[wide, wide, pl.BlockSpec((4 * order, rows), lambda i: (0, i))],
         out_shape=[
             jax.ShapeDtypeStruct((channels, chunk), jnp.float32),
             jax.ShapeDtypeStruct((channels, chunk), jnp.float32),
-            jax.ShapeDtypeStruct((channels, 4 * order), jnp.float32),
+            jax.ShapeDtypeStruct((4 * order, channels), jnp.float32),
         ],
     )(keys, values, cotangent, queries, dec, weight)
 
@@ -97,6 +109,7 @@
     conv_intra, back_intra, stats = chunk_pass(
         keys[0], values[0], cotangent[0], queries[0], dec, weight, length
     )
+    stats = stats.reshape(order, 4, channels).transpose(2, 1, 0).reshape(channels, 4 * order)
     lead_fwd = jnp.exp(-dk * ((pos + 1) / length))
     lead_bwd = jnp.exp(-dk * ((chunk - pos) / length))
 

time: 219 us -> 193 us (0.88)
  Pallas kernels: 69 us -> 38.2 us
  local copies, waits for them, and re-layouts: 12.1 us -> 18.4 us
    pallas_call x1, Pallas kernels: 69 us -> 38.2 us  [chunk_pass(): pl.pallas_call(functools.partial(chunk_kernel, length=length), grid=(chan...]
    another operation x0 -> x2, local copies, waits for them, and re-layouts: none -> 4.2 us  [body(): stats = stats.reshape(n_dp, n_ctx, groups, 4 * order)]
    reshape x1 -> x2, local copies, waits for them, and re-layouts: 1.51 us -> 4.27 us  [body(): stats.reshape(order, 4, channels).transpose(2, 1, 0)]
  transfers between devices with their start and end apart: 3 -> 3, of which waited for: 3 -> 3; matrix products, arithmetic and copies ran while one was open for 2% -> 3% of each run, Pallas kernels for 0% -> 0%
where the time goes in v2:
time: 193 us; the launch traced here: 192 us
  blocking collectives  47.9 us (25%)
  Pallas kernels  38.2 us (20%)
  other arithmetic  36 us (19%)
  waiting for transfers between devices  34.2 us (18%)
  local copies, waits for them, and re-layouts  18.4 us (10%)
  starting transfers between devices  16.6 us (9%)
    pallas_call x1, Pallas kernels, chunk_pass(): pl.pallas_call(functools.partial(chunk_kernel, length=length), grid=(chan...  38.2 us
    all_to_all x1, blocking collectives, body(): lax.all_to_all(jnp.broadcast_to(own[None], (n_dp,) + own.shape), 'dp', 0,...  28.2 us
    all_to_all x1, blocking collectives, body(): lax.all_to_all(jnp.broadcast_to(part, (n_dp, n_ctx, block, 2 * order)), '...  19.7 us
    all_to_all x1, waiting for transfers between devices, body(): stats = lax.all_to_all(stats, 'ctx', 1, 1, tiled=True)  16.2 us
    reduce_sum x1, other arithmetic, body(): jnp.sum((weight * carry_bwd)[:, :, None] * lead_bwd, axis=1)  14.5 us
    all_to_all x1, waiting for transfers between devices, body(): lax.all_to_all(jnp.concatenate([carry_fwd, carry_bwd], axis=-1), 'ctx', 1...  10.2 us
    all_to_all x1, waiting for transfers between devices, body(): total = jnp.sum(lax.all_to_all(cross_grp, 'dp', 0, 0, tiled=True), axis=0)  7.73 us
    unnamed x27, local copies, waits for them, and re-layouts  7.31 us
  transfers between devices with their start and end apart: 3, of which 3 were waited for; matrix products, arithmetic and copies ran while one was open for 3% of the time, Pallas kernels for 0%

profile of v2, /device:TPU:1, one launch (start us, length us, event | category | flops | bytes accessed | tf_op | source)
XLA Modules:
  0.0 192.1 jit_solution(13882776526371796023)
XLA Ops:
  0.6 0.8 pad_maximum_fusion.1
  1.5 28.2 %all_to_all.25 = f32[8,1,128]{2,1,0:T(1,128)S(1)} all-to-all(f32[8,1,128]{2,1,0:T(1,128)S(1)} %reshape.45), channel_id=1, replica_groups=mesh['dp'=8,'ctx'=64] {'dp'}, dimensions={0} | all-to-all | bytes 8192 | tf_op jit(solution)/shard_map/all_to_all | solution.py:97
  31.9 19.7 %all_to_all.26 = f32[64,1,1024]{2,1,0:T(1,128)S(1)} all-to-all(f32[64,1,1024]{2,1,0:T(1,128)S(1)} %reshape.47), channel_id=1, replica_groups=mesh['dp'=8,'ctx'=64] {'ctx'}, dimensions={0} | all-to-all | bytes 524288 | tf_op jit(solution)/shard_map/all_to_all | solution.py:100
  51.5 1.3 reduce.1
  53.5 2.2 %slice_negate_fusion = (f32[2048,16]{1,0:T(8,128)}, f32[2048,16]{1,0:T(8,128)}, f32[2048,16]{1,0:T(8,128)}) fusion(f32[2048,32]{1,0:T(8,128)S(1)} %bitcast.41), kind=kLoop, calls=%fused_computation.46 | loop fusion | flops 131072 | bytes 655360 | tf_op jit(solution)/shard_map/neg | solution.py:113
  55.8 38.2 %shard_map.101 = (f32[2048,128]{1,0:T(8,128)}, f32[2048,128]{1,0:T(8,128)}, f32[64,2048]{1,0:T(8,128)}) custom-call(bf16[2048,128]{1,0:T(8,128)(2,1)} %bitcast.48, bf16[2048,128]{1,0:T(8,128)(2,1)} %bitcast.50, bf16[2048,128]{1,0:T(8,128)(2,1)} %bitcast.47, bf16[2048,128]{1,0:T(8,128)(2,1)} %bitcast.49, f32[2048,16]{1,0:T(8,128)} %get-tuple-element.23.dec_ref, ...), custom_call_target="tpu_custom_call" | custom-call | tf_op jit(solution)/shard_map/pallas_call | solution.py:74
  93.9 1.2 reshape.40
  95.1 3.1 %copy.22 = f32[16,4,2048]{0,1,2:T(4,128)} copy(f32[16,4,2048]{2,1,0:T(4,128)S(1)} %reshape.40) | data formatting | bytes 1048576 | tf_op jit(solution)/shard_map/reshape | solution.py:112
  98.2 3.9 %reshape_reshape.3 = f32[8,64,4,64]{3,2,1,0:T(4,128)S(1)} reshape(f32[2048,4,16]{2,1,0:T(4,128)} %bitcast.40) | data formatting | bytes 1048576 | tf_op jit(solution)/shard_map/reshape;reshape | solution.py:117
  102.4 1.8 reshape.49
  104.2 6.3 %all-to-all-start.2 = ((f32[64,1,2048]{2,1,0:T(1,128)}), f32[64,1,2048]{2,1,0:T(1,128)S(1)}, u32[]{:S(2)}, u32[]{:S(2)}) async-start(f32[64,1,2048]{2,1,0:T(1,128)} %reshape.49), calls=%async_computation.2 | async-start | bytes 1048576 | tf_op jit(solution)/shard_map/all_to_all | solution.py:118
  110.5 0.8 exponential_bitcast_fusion
  111.2 16.2 %all-to-all-done.2 = f32[64,1,2048]{2,1,0:T(1,128)S(1)} async-done(((f32[64,1,2048]{2,1,0:T(1,128)}), f32[64,1,2048]{2,1,0:T(1,128)S(1)}, u32[]{:S(2)}, u32[]{:S(2)}) %all-to-all-start.2) | async-done | bytes 524320 | tf_op jit(solution)/shard_map/all_to_all | solution.py:118
  127.5 1.9 reduce.2
  129.3 0.7 reshape.50
  131.2 1.0 multiply_add_fusion.11
  132.4 1.0 multiply_add_fusion.10
  133.6 1.0 multiply_add_fusion.9
  134.7 1.1 multiply_add_fusion.8
  136.0 0.9 multiply_add_fusion.7
  137.0 1.8 fusion.5
  138.8 5.6 %all-to-all-start.4 = ((f32[8,4,16]{2,1,0:T(4,128)}), f32[8,4,16]{2,1,0:T(4,128)S(1)}, u32[]{:S(2)}, u32[]{:S(2)}) async-start(f32[8,4,16]{2,1,0:T(4,128)} %get-tuple-element.13), calls=%async_computation.4 | async-start | bytes 32768 | tf_op jit(solution)/shard_map/all_to_all | solution.py:153
  144.4 1.6 fusion.11
  146.0 2.6 %reshape.51 = f32[64,1,1024]{2,1,0:T(1,128)} reshape(f32[64,8,4,32]{3,2,1,0:T(4,128)} %fusion.11) | data formatting | bytes 524288
  148.6 7.7 %all-to-all-done.4 = f32[8,4,16]{2,1,0:T(4,128)S(1)} async-done(((f32[8,4,16]{2,1,0:T(4,128)}), f32[8,4,16]{2,1,0:T(4,128)S(1)}, u32[]{:S(2)}, u32[]{:S(2)}) %all-to-all-start.4) | async-done | bytes 2080 | tf_op jit(solution)/shard_map/all_to_all | solution.py:153
  156.3 4.7 %all-to-all-start.3 = ((f32[64,1,1024]{2,1,0:T(1,128)}), f32[64,1,1024]{2,1,0:T(1,128)S(1)}, u32[]{:S(2)}, u32[]{:S(2)}) async-start(f32[64,1,1024]{2,1,0:T(1,128)} %reshape.51), calls=%async_computation.3 | async-start | bytes 524288 | tf_op jit(solution)/shard_map/all_to_all | solution.py:148
  161.6 10.2 %all-to-all-done.3 = f32[64,1,1024]{2,1,0:T(1,128)S(1)} async-done(((f32[64,1,1024]{2,1,0:T(1,128)}), f32[64,1,1024]{2,1,0:T(1,128)S(1)}, u32[]{:S(2)}, u32[]{:S(2)}) %all-to-all-start.3) | async-done | bytes 262176 | tf_op jit(solution)/shard_map/all_to_all | solution.py:148
  171.8 1.3 reduce.3
  174.3 14.5 %multiply_reduce_fusion = (f32[2048,128]{1,0:T(8,128)S(1)}, f32[2048,128]{1,0:T(8,128)S(1)}) fusion(f32[128]{0:T(128)S(1)} %subtract_multiply_fusion, f32[2048,16]{1,0:T(8,128)S(1)} %get-tuple-element.20, f32[2048,16]{1,0:T(8,128)S(1)} %copy-done.7, f32[128]{0:T(128)S(1)} %add_multiply_fusion, f32[2048,16]{1,0:T(8,128)S(1)} %get-tuple-element.19), kind=kLoop, calls=%fused_computation | loop fusion | flops 24641536 | bytes 2491392 | tf_op jit(solution)/shard_map/reduce_sum | solution.py:159
  188.9 1.3 fusion.1
  190.2 0.9 fusion
  191.2 0.9 fusion.2
  (48 shorter events, 6.8 us)
Async XLA Ops:
  104.2 23.3 %all-to-all-start.2 = ((f32[64,1,2048]{2,1,0:T(1,128)}), f32[64,1,2048]{2,1,0:T(1,128)S(1)}, u32[]{:S(2)}, u32[]{:S(2)}) async-start(f32[64,1,2048]{2,1,0:T(1,128)} %reshape.49), calls=%async_computation.2 | async-start | bytes 1048576 | tf_op jit(solution)/shard_map/all_to_all | solution.py:118
  138.8 22.2 %copy-start.8 = (f32[4,16]{1,0:T(4,128)S(1)}, f32[4,16]{1,0:T(4,128)}, u32[]{:S(2)}) copy-start(f32[4,16]{1,0:T(4,128)} %param.11) | copy-start | bytes 772
  138.8 17.5 %all-to-all-start.4 = ((f32[8,4,16]{2,1,0:T(4,128)}), f32[8,4,16]{2,1,0:T(4,128)S(1)}, u32[]{:S(2)}, u32[]{:S(2)}) async-start(f32[8,4,16]{2,1,0:T(4,128)} %get-tuple-element.13), calls=%async_computation.4 | async-start | bytes 32768 | tf_op jit(solution)/shard_map/all_to_all | solution.py:153
  144.4 29.4 %copy-start = (f32[2048,16]{1,0:T(8,128)S(1)}, f32[2048,16]{1,0:T(8,128)}, u32[]{:S(2)}) copy-start(f32[2048,16]{1,0:T(8,128)} %get-tuple-element.22.w_ref) | copy-start | bytes 393220
  156.3 15.5 %all-to-all-start.3 = ((f32[64,1,1024]{2,1,0:T(1,128)}), f32[64,1,1024]{2,1,0:T(1,128)S(1)}, u32[]{:S(2)}, u32[]{:S(2)}) async-start(f32[64,1,1024]{2,1,0:T(1,128)} %reshape.51), calls=%async_computation.3 | async-start | bytes 524288 | tf_op jit(solution)/shard_map/all_to_all | solution.py:148
  173.1 1.2 copy-start.7
  174.3 14.5 %copy-start.1 = (bf16[1,2048,128]{2,1,0:T(8,128)(2,1)S(1)}, bf16[1,2048,128]{2,1,0:T(8,128)(2,1)}, u32[]{:S(2)}) copy-start(bf16[1,2048,128]{2,1,0:T(8,128)(2,1)} %param.9) | copy-start | bytes 1572868
  174.3 14.6 %copy-start.2 = (bf16[1,2048,128]{2,1,0:T(8,128)(2,1)S(1)}, bf16[1,2048,128]{2,1,0:T(8,128)(2,1)}, u32[]{:S(2)}) copy-start(bf16[1,2048,128]{2,1,0:T(8,128)(2,1)} %param.7) | copy-start | bytes 1572868
  174.3 14.6 %copy-start.5 = (f32[2048,128]{1,0:T(8,128)S(1)}, f32[2048,128]{1,0:T(8,128)}, u32[]{:S(2)}) copy-start(f32[2048,128]{1,0:T(8,128)} %get-tuple-element.8) | copy-start | bytes 3145732
  174.3 14.6 %copy-start.6 = (f32[2048,128]{1,0:T(8,128)S(1)}, f32[2048,128]{1,0:T(8,128)}, u32[]{:S(2)}) copy-start(f32[2048,128]{1,0:T(8,128)} %get-tuple-element.10) | copy-start | bytes 3145732
  188.9 1.4 copy-start.3
  188.9 2.3 %copy-start.4 = (bf16[1,2048,128]{2,1,0:T(8,128)(2,1)S(1)}, bf16[1,2048,128]{2,1,0:T(8,128)(2,1)}, u32[]{:S(2)}) copy-start(bf16[1,2048,128]{2,1,0:T(8,128)(2,1)} %param.8) | copy-start | bytes 1572868

commit v3 on v2

--- a/solution.py
+++ b/solution.py
@@ -110,8 +110,9 @@
         keys[0], values[0], cotangent[0], queries[0], dec, weight, length
     )
     stats = stats.reshape(order, 4, channels).transpose(2, 1, 0).reshape(channels, 4 * order)
-    lead_fwd = jnp.exp(-dk * ((pos + 1) / length))
-    lead_bwd = jnp.exp(-dk * ((chunk - pos) / length))
+    sub = 16
+    outer = jnp.arange(chunk // sub, dtype=f32) * sub
+    inner = jnp.arange(sub, dtype=f32)
 
     groups = channels // (n_dp * n_ctx)
     stats = stats.reshape(n_dp, n_ctx, groups, 4 * order)
@@ -155,8 +156,14 @@
     own_scale = jnp.sqrt(1.0 - jnp.exp(-2.0 * decays / length))
     grad_residues = total * own_scale / math.sqrt(seq_count * n_dp * length)
 
-    conv_full = conv_intra + jnp.sum((weight * carry_fwd)[:, :, None] * lead_fwd, axis=1)
-    back_full = back_intra + jnp.sum((weight * carry_bwd)[:, :, None] * lead_bwd, axis=1)
+    fwd_outer = (weight * carry_fwd)[:, :, None] * jnp.exp(-dk * (outer / length))
+    fwd_inner = jnp.exp(-dk * ((inner + 1) / length))
+    bwd_outer = (weight * carry_bwd)[:, :, None] * jnp.exp(-dk * ((chunk - outer) / length))
+    bwd_inner = jnp.exp(dk * (inner / length))
+    conv_carry = jnp.sum(fwd_outer[:, :, :, None] * fwd_inner[:, :, None, :], axis=1)
+    back_carry = jnp.sum(bwd_outer[:, :, :, None] * bwd_inner[:, :, None, :], axis=1)
+    conv_full = conv_intra + conv_carry.reshape(channels, chunk)
+    back_full = back_intra + back_carry.reshape(channels, chunk)
     conv_f = conv_full.astype(jnp.bfloat16).astype(f32)[None]
     back_f = back_full.astype(jnp.bfloat16).astype(f32)[None]
     mixed = (queries.astype(f32) * conv_f).astype(jnp.bfloat16)

time: 193 us -> 202 us (1.047)
  local copies, waits for them, and re-layouts: 18.4 us -> 28.9 us
  other arithmetic: 36 us -> 33.1 us
    reduce_sum x1 -> x2, other arithmetic: 14.5 us -> 6.09 us  [the longest x1 3.68 us: body(): jnp.sum(fwd_outer[:, :, :, None] * fwd_inner[:, :, None, :], axis=1)]
    reshape x0 -> x2, local copies, waits for them, and re-layouts: none -> 3.09 us  [the longest x1 1.55 us: body(): back_full = back_intra + back_carry.reshape(channels, chunk)]
    mul x0 -> x2, local copies, waits for them, and re-layouts: none -> 3.05 us  [the longest x1 1.53 us: body(): weight * carry_bwd]
    mul x1 -> x2, other arithmetic: 0.38 us -> 2.97 us  [the longest x1 1.62 us: body(): weight * carry_bwd]
    all_to_all x1, waiting for transfers between devices: 7.73 us -> 9.91 us  [body(): total = jnp.sum(lax.all_to_all(cross_grp, 'dp', 0, 0, tiled=True), axis=0)]
    exp x0 -> x2, other arithmetic: none -> 2.11 us  [the longest x1 1.69 us: body(): bwd_inner = jnp.exp(dk * (inner / length))]
    unnamed x27 -> x21, local copies, waits for them, and re-layouts: 7.31 us -> 8.83 us
where the time goes in v3:
time: 202 us; the launch traced here: 201 us
  blocking collectives  47.9 us (24%)
  Pallas kernels  38.2 us (19%)
  waiting for transfers between devices  34.4 us (17%)
  other arithmetic  33.1 us (16%)
  local copies, waits for them, and re-layouts  28.9 us (14%)
  starting transfers between devices  17.2 us (9%)
    pallas_call x1, Pallas kernels, chunk_pass(): pl.pallas_call(functools.partial(chunk_kernel, length=length), grid=(chan...  38.2 us
    all_to_all x1, blocking collectives, body(): lax.all_to_all(jnp.broadcast_to(own[None], (n_dp,) + own.shape), 'dp', 0,...  28.2 us
    all_to_all x1, blocking collectives, body(): lax.all_to_all(jnp.broadcast_to(part, (n_dp, n_ctx, block, 2 * order)), '...  19.7 us
    all_to_all x1, waiting for transfers between devices, body(): stats = lax.all_to_all(stats, 'ctx', 1, 1, tiled=True)  16.3 us
    all_to_all x1, waiting for transfers between devices, body(): total = jnp.sum(lax.all_to_all(cross_grp, 'dp', 0, 0, tiled=True), axis=0)  9.91 us
    unnamed x21, local copies, waits for them, and re-layouts  8.83 us
    all_to_all x1, waiting for transfers between devices, body(): lax.all_to_all(jnp.concatenate([carry_fwd, carry_bwd], axis=-1), 'ctx', 1...  8.25 us
    all_to_all x1, starting transfers between devices, body(): stats = lax.all_to_all(stats, 'ctx', 1, 1, tiled=True)  6.28 us
  transfers between devices with their start and end apart: 3, of which 3 were waited for; matrix products, arithmetic and copies ran while one was open for 3% of the time, Pallas kernels for 0%

profile of v3, /device:TPU:1, one launch (start us, length us, event | category | flops | bytes accessed | tf_op | source)
XLA Modules:
  0.0 200.7 jit_solution(8366504742649299021)
XLA Ops:
  1.5 28.2 %all_to_all.25 = f32[8,1,128]{2,1,0:T(1,128)S(1)} all-to-all(f32[8,1,128]{2,1,0:T(1,128)S(1)} %reshape.73), channel_id=1, replica_groups=mesh['dp'=8,'ctx'=64] {'dp'}, dimensions={0} | all-to-all | bytes 8192 | tf_op jit(solution)/shard_map/all_to_all | solution.py:97
  31.9 19.7 %all_to_all.26 = f32[64,1,1024]{2,1,0:T(1,128)S(1)} all-to-all(f32[64,1,1024]{2,1,0:T(1,128)S(1)} %reshape.75), channel_id=1, replica_groups=mesh['dp'=8,'ctx'=64] {'ctx'}, dimensions={0} | all-to-all | bytes 524288 | tf_op jit(solution)/shard_map/all_to_all | solution.py:100
  51.5 1.3 reduce.1
  53.5 1.8 slice_negate_fusion
  55.4 38.2 %shard_map.101 = (f32[2048,128]{1,0:T(8,128)}, f32[2048,128]{1,0:T(8,128)}, f32[64,2048]{1,0:T(8,128)}) custom-call(bf16[2048,128]{1,0:T(8,128)(2,1)} %bitcast.52, bf16[2048,128]{1,0:T(8,128)(2,1)} %bitcast.54, bf16[2048,128]{1,0:T(8,128)(2,1)} %bitcast.51, bf16[2048,128]{1,0:T(8,128)(2,1)} %bitcast.53, f32[2048,16]{1,0:T(8,128)} %get-tuple-element.29.dec_ref, ...), custom_call_target="tpu_custom_call" | custom-call | tf_op jit(solution)/shard_map/pallas_call | solution.py:74
  93.5 1.2 reshape.66
  94.7 3.1 %copy.46 = f32[16,4,2048]{0,1,2:T(4,128)} copy(f32[16,4,2048]{2,1,0:T(4,128)S(1)} %reshape.66) | data formatting | bytes 1048576 | tf_op jit(solution)/shard_map/reshape | solution.py:112
  97.8 3.9 %reshape_reshape.3 = f32[8,64,4,64]{3,2,1,0:T(4,128)S(1)} reshape(f32[2048,4,16]{2,1,0:T(4,128)} %bitcast.42) | data formatting | bytes 1048576 | tf_op jit(solution)/shard_map/reshape;reshape | solution.py:118
  101.7 1.3 copy.59
  103.0 3.0 %reshape.77 = f32[64,1,2048]{2,1,0:T(1,128)} reshape(f32[64,8,4,64]{3,2,1,0:T(4,128)} %bitcast.48) | data formatting | bytes 1048576
  106.0 6.3 %all-to-all-start.2 = ((f32[64,1,2048]{2,1,0:T(1,128)}), f32[64,1,2048]{2,1,0:T(1,128)S(1)}, u32[]{:S(2)}, u32[]{:S(2)}) async-start(f32[64,1,2048]{2,1,0:T(1,128)} %reshape.77), calls=%async_computation.2 | async-start | bytes 1048576 | tf_op jit(solution)/shard_map/all_to_all | solution.py:119
  113.0 16.3 %all-to-all-done.2 = f32[64,1,2048]{2,1,0:T(1,128)S(1)} async-done(((f32[64,1,2048]{2,1,0:T(1,128)}), f32[64,1,2048]{2,1,0:T(1,128)S(1)}, u32[]{:S(2)}, u32[]{:S(2)}) %all-to-all-start.2) | async-done | bytes 524320 | tf_op jit(solution)/shard_map/all_to_all | solution.py:119
  129.2 1.9 reduce.2
  138.8 1.8 fusion.5
  140.6 5.5 %all-to-all-start.4 = ((f32[8,4,16]{2,1,0:T(4,128)}), f32[8,4,16]{2,1,0:T(4,128)S(1)}, u32[]{:S(2)}, u32[]{:S(2)}) async-start(f32[8,4,16]{2,1,0:T(4,128)} %get-tuple-element.11), calls=%async_computation.4 | async-start | bytes 32768 | tf_op jit(solution)/shard_map/all_to_all | solution.py:154
  146.7 1.4 reshape.79
  148.1 9.9 %all-to-all-done.4 = f32[8,4,16]{2,1,0:T(4,128)S(1)} async-done(((f32[8,4,16]{2,1,0:T(4,128)}), f32[8,4,16]{2,1,0:T(4,128)S(1)}, u32[]{:S(2)}, u32[]{:S(2)}) %all-to-all-start.4) | async-done | bytes 2080 | tf_op jit(solution)/shard_map/all_to_all | solution.py:154
  158.0 5.5 %all-to-all-start.3 = ((f32[64,1,1024]{2,1,0:T(1,128)}), f32[64,1,1024]{2,1,0:T(1,128)}, u32[]{:S(2)}, u32[]{:S(2)}) async-start(f32[64,1,1024]{2,1,0:T(1,128)} %reshape.79), calls=%async_computation.3 | async-start | bytes 524288 | tf_op jit(solution)/shard_map/all_to_all | solution.py:149
  163.5 1.7 multiply_exponential_fusion
  166.2 8.2 %all-to-all-done.3 = f32[64,1,1024]{2,1,0:T(1,128)} async-done(((f32[64,1,1024]{2,1,0:T(1,128)}), f32[64,1,1024]{2,1,0:T(1,128)}, u32[]{:S(2)}, u32[]{:S(2)}) %all-to-all-start.3) | async-done | bytes 262176 | tf_op jit(solution)/shard_map/all_to_all | solution.py:149
  174.5 2.2 %reduce.3 = f32[64,1024]{1,0:T(8,128)S(1)} reduce(f32[64,1,1024]{2,1,0:T(1,128)} %all-to-all-done.3, f32[]{:T(128)} %broadcast.170), dimensions={1}, to_apply=%all_to_all.18.reduce_sub_computation | reduce | bytes 524292 | tf_op jit(solution)/shard_map/all_to_all | solution.py:149
  176.7 1.5 reshape.80
  178.2 1.4 copy.48
  179.7 1.6 slice_multiply_fusion.1
  181.3 1.5 copy.49
  182.8 1.5 copy.53
  184.3 1.3 exponential_multiply_fusion
  186.3 2.4 %multiply_reduce_fusion = f32[2048,8,16]{0,2,1:T(8,128)} fusion(f32[2048,16,16]{0,2,1:T(8,128)S(1)} %copy-done.2, f32[2048,16,8]{0,2,1:T(8,128)S(1)} %get-tuple-element.30), kind=kLoop, calls=%fused_computation | loop fusion | flops 8126464 | bytes 4194304 | tf_op jit(solution)/shard_map/reduce_sum | solution.py:164
  188.7 1.5 copy.55
  190.3 3.7 %multiply_reduce_fusion.1 = f32[2048,8,16]{0,2,1:T(8,128)} fusion(f32[2048,16,16]{0,2,1:T(8,128)S(1)} %multiply_exponential_fusion.1, f32[2048,16,8]{0,2,1:T(8,128)} %get-tuple-element.31), kind=kLoop, calls=%fused_computation.1 | loop fusion | flops 8126464 | bytes 4194304 | tf_op jit(solution)/shard_map/reduce_sum | solution.py:163
  194.0 1.5 copy.52
  195.5 3.3 %fusion.1 = (bf16[1,2048,128]{2,1,0:T(8,128)(2,1)}, bf16[1,2048,128]{2,1,0:T(8,128)(2,1)S(1)}, bf16[1,2048,128]{2,1,0:T(8,128)(2,1)}, bf16[1,2048,128]{2,1,0:T(8,128)(2,1)S(1)}) fusion(bf16[1,2048,128]{2,1,0:T(8,128)(2,1)} %param.9, f32[2048,128]{1,0:T(8,128)} %get-tuple-element.8, f32[2048,128]{1,0:T(8,128)S(1)} %copy.52, bf16[1,2048,128]{2,1,0:T(8,128)(2,1)} %param.7, ...), kind=kLoop, calls=%fused_computation.9 | loop fusion | flops 3145728 | bytes 7340032 | tf_op jit(solution)/shard_map/convert_element_type | solution.py:170
  (54 shorter events, 16.1 us)
Async XLA Ops:
  101.7 10.6 %copy-start = (f32[2048,16]{1,0:T(8,128)S(1)}, f32[2048,16]{1,0:T(8,128)}, u32[]{:S(2)}) copy-start(f32[2048,16]{1,0:T(8,128)} %get-tuple-element.29.dec_ref) | copy-start | bytes 393220
  106.0 23.3 %all-to-all-start.2 = ((f32[64,1,2048]{2,1,0:T(1,128)}), f32[64,1,2048]{2,1,0:T(1,128)S(1)}, u32[]{:S(2)}, u32[]{:S(2)}) async-start(f32[64,1,2048]{2,1,0:T(1,128)} %reshape.77), calls=%async_computation.2 | async-start | bytes 1048576 | tf_op jit(solution)/shard_map/all_to_all | solution.py:119
  140.6 17.4 %all-to-all-start.4 = ((f32[8,4,16]{2,1,0:T(4,128)}), f32[8,4,16]{2,1,0:T(4,128)S(1)}, u32[]{:S(2)}, u32[]{:S(2)}) async-start(f32[8,4,16]{2,1,0:T(4,128)} %get-tuple-element.11), calls=%async_computation.4 | async-start | bytes 32768 | tf_op jit(solution)/shard_map/all_to_all | solution.py:154
  158.0 16.5 %all-to-all-start.3 = ((f32[64,1,1024]{2,1,0:T(1,128)}), f32[64,1,1024]{2,1,0:T(1,128)}, u32[]{:S(2)}, u32[]{:S(2)}) async-start(f32[64,1,1024]{2,1,0:T(1,128)} %reshape.79), calls=%async_computation.3 | async-start | bytes 524288 | tf_op jit(solution)/shard_map/all_to_all | solution.py:149
  163.5 2.2 %copy-start.5 = (f32[4,16]{1,0:T(4,128)S(1)}, f32[4,16]{1,0:T(4,128)}, u32[]{:S(2)}) copy-start(f32[4,16]{1,0:T(4,128)} %param.11) | copy-start | bytes 772
  165.6 14.1 %copy-start.1 = (f32[2048,16]{1,0:T(8,128)S(1)}, f32[2048,16]{1,0:T(8,128)}, u32[]{:S(2)}) copy-start(f32[2048,16]{1,0:T(8,128)} %get-tuple-element.28.w_ref) | copy-start | bytes 393220
  184.3 2.0 copy-start.2
  195.5 3.3 %copy-start.3 = (bf16[1,2048,128]{2,1,0:T(8,128)(2,1)S(1)}, bf16[1,2048,128]{2,1,0:T(8,128)(2,1)}, u32[]{:S(2)}) copy-start(bf16[1,2048,128]{2,1,0:T(8,128)(2,1)} %param.6) | copy-start | bytes 1572868
  195.5 4.2 %copy-start.4 = (bf16[1,2048,128]{2,1,0:T(8,128)(2,1)S(1)}, bf16[1,2048,128]{2,1,0:T(8,128)(2,1)}, u32[]{:S(2)}) copy-start(bf16[1,2048,128]{2,1,0:T(8,128)(2,1)} %param.8) | copy-start | bytes 1572868

commit v4 on v2

--- a/solution.py
+++ b/solution.py
@@ -109,47 +109,47 @@
     conv_intra, back_intra, stats = chunk_pass(
         keys[0], values[0], cotangent[0], queries[0], dec, weight, length
     )
-    stats = stats.reshape(order, 4, channels).transpose(2, 1, 0).reshape(channels, 4 * order)
     lead_fwd = jnp.exp(-dk * ((pos + 1) / length))
     lead_bwd = jnp.exp(-dk * ((chunk - pos) / length))
 
     groups = channels // (n_dp * n_ctx)
-    stats = stats.reshape(n_dp, n_ctx, groups, 4 * order)
-    stats = lax.all_to_all(stats, "ctx", 1, 1, tiled=True)
-    s_fwd = stats[..., :order]
-    s_bwd = stats[..., order : 2 * order]
-    c_intra = stats[..., 2 * order : 3 * order]
-    c_lead = stats[..., 3 * order :]
+    stats = lax.all_to_all(
+        stats.reshape(order, 4, n_dp, n_ctx, groups), "ctx", 3, 3, tiled=True
+    )
+    s_fwd = stats[:, 0]
+    s_bwd = stats[:, 1]
+    c_intra = stats[:, 2]
+    c_lead = stats[:, 3]
     dec_grp = lax.dynamic_slice_in_dim(
         dec.reshape(n_dp, n_ctx, groups, order), ctx_at, 1, axis=1
-    )
+    ).transpose(3, 0, 1, 2)
     hop_decay = dec_grp * (chunk / length)
 
     def exclusive_scan(state, sign):
-        pad = jnp.zeros_like(state[:, :1])
+        pad = jnp.zeros_like(state[:, :, :1])
         if sign > 0:
-            carry = jnp.concatenate([pad, state[:, :-1]], axis=1)
+            carry = jnp.concatenate([pad, state[:, :, :-1]], axis=2)
         else:
-            carry = jnp.concatenate([state[:, 1:], pad], axis=1)
+            carry = jnp.concatenate([state[:, :, 1:], pad], axis=2)
         hop = 1
         while hop < n_ctx:
-            fill = jnp.zeros_like(carry[:, :hop])
+            fill = jnp.zeros_like(carry[:, :, :hop])
             if sign > 0:
-                moved = jnp.concatenate([fill, carry[:, :-hop]], axis=1)
+                moved = jnp.concatenate([fill, carry[:, :, :-hop]], axis=2)
             else:
-                moved = jnp.concatenate([carry[:, hop:], fill], axis=1)
+                moved = jnp.concatenate([carry[:, :, hop:], fill], axis=2)
             carry = carry + jnp.exp(-hop_decay * hop) * moved
             hop *= 2
         return carry
 
     carry_fwd = exclusive_scan(s_fwd, 1)
     carry_bwd = exclusive_scan(s_bwd, -1)
-    cross_grp = jnp.sum(c_intra + carry_fwd * c_lead, axis=1)
+    cross_grp = jnp.sum(c_intra + carry_fwd * c_lead, axis=2).transpose(1, 2, 0)
     carries = lax.all_to_all(
-        jnp.concatenate([carry_fwd, carry_bwd], axis=-1), "ctx", 1, 1, tiled=True
-    ).reshape(channels, 2 * order)
-    carry_fwd = carries[:, :order]
-    carry_bwd = carries[:, order:]
+        jnp.concatenate([carry_fwd, carry_bwd], axis=0), "ctx", 2, 2, tiled=True
+    ).reshape(2 * order, channels)
+    carry_fwd = carries[:order].T
+    carry_bwd = carries[order:].T
     total = jnp.sum(lax.all_to_all(cross_grp, "dp", 0, 0, tiled=True), axis=0)
 
     own_scale = jnp.sqrt(1.0 - jnp.exp(-2.0 * decays / length))

time: 193 us -> 224 us (1.16)
  local copies, waits for them, and re-layouts: 18.4 us -> 51.9 us
  other arithmetic: 36 us -> 32.9 us
    reshape x2, local copies, waits for them, and re-layouts: 4.27 us -> 35.4 us  [body(): stats.reshape(order, 4, n_dp, n_ctx, groups)]
    unnamed x27, local copies, waits for them, and re-layouts: 7.31 us -> 11.6 us
    another operation x2 -> x0, local copies, waits for them, and re-layouts: 4.2 us -> none  [body(): stats = stats.reshape(n_dp, n_ctx, groups, 4 * order)]
    add x5, other arithmetic: 5.07 us -> 2.43 us  [exclusive_scan(): carry = carry + jnp.exp(-hop_decay * hop) * moved]
  transfers between devices with their start and end apart: 3 -> 3, of which waited for: 3 -> 3; matrix products, arithmetic and copies ran while one was open for 3% -> 2% of each run, Pallas kernels for 0% -> 0%
where the time goes in v4:
time: 224 us; the launch traced here: 223 us
  local copies, waits for them, and re-layouts  51.9 us (23%)
  blocking collectives  47.9 us (21%)
  Pallas kernels  38.2 us (17%)
  waiting for transfers between devices  34.3 us (15%)
  other arithmetic  32.9 us (15%)
  starting transfers between devices  16.8 us (8%)
    pallas_call x1, Pallas kernels, chunk_pass(): pl.pallas_call(functools.partial(chunk_kernel, length=length), grid=(chan...  38.2 us
    reshape x2, local copies, waits for them, and re-layouts, body(): stats.reshape(order, 4, n_dp, n_ctx, groups)  35.4 us
    all_to_all x1, blocking collectives, body(): lax.all_to_all(jnp.broadcast_to(own[None], (n_dp,) + own.shape), 'dp', 0,...  28.2 us
    all_to_all x1, blocking collectives, body(): lax.all_to_all(jnp.broadcast_to(part, (n_dp, n_ctx, block, 2 * order)), '...  19.7 us
    all_to_all x1, waiting for transfers between devices, body(): lax.all_to_all(stats.reshape(order, 4, n_dp, n_ctx, groups), 'ctx', 3, 3,...  16.2 us
    reduce_sum x1, other arithmetic, body(): jnp.sum((weight * carry_bwd)[:, :, None] * lead_bwd, axis=1)  15.6 us
    unnamed x27, local copies, waits for them, and re-layouts  11.6 us
    all_to_all x1, waiting for transfers between devices, body(): lax.all_to_all(jnp.concatenate([carry_fwd, carry_bwd], axis=0), 'ctx', 2,...  9.99 us
  transfers between devices with their start and end apart: 3, of which 3 were waited for; matrix products, arithmetic and copies ran while one was open for 2% of the time, Pallas kernels for 0%

profile of v4, /device:TPU:1, one launch (start us, length us, event | category | flops | bytes accessed | tf_op | source)
XLA Modules:
  0.0 223.0 jit_solution(8251270949362222931)
XLA Ops:
  0.6 0.8 pad_maximum_fusion.1
  1.5 28.2 %all_to_all.25 = f32[8,1,128]{2,1,0:T(1,128)S(1)} all-to-all(f32[8,1,128]{2,1,0:T(1,128)S(1)} %reshape.44), channel_id=1, replica_groups=mesh['dp'=8,'ctx'=64] {'dp'}, dimensions={0} | all-to-all | bytes 8192 | tf_op jit(solution)/shard_map/all_to_all | solution.py:97
  30.2 0.7 reduce
  31.2 0.7 reshape.46
  31.9 19.7 %all_to_all.26 = f32[64,1,1024]{2,1,0:T(1,128)S(1)} all-to-all(f32[64,1,1024]{2,1,0:T(1,128)S(1)} %reshape.46), channel_id=1, replica_groups=mesh['dp'=8,'ctx'=64] {'ctx'}, dimensions={0} | all-to-all | bytes 524288 | tf_op jit(solution)/shard_map/all_to_all | solution.py:100
  51.5 1.3 reduce.1
  52.8 0.5 reshape.47
  53.5 2.2 slice_negate_fusion
  55.8 38.2 %shard_map.101 = (f32[2048,128]{1,0:T(8,128)}, f32[2048,128]{1,0:T(8,128)}, f32[64,2048]{1,0:T(8,128)}) custom-call(bf16[2048,128]{1,0:T(8,128)(2,1)} %bitcast.85, bf16[2048,128]{1,0:T(8,128)(2,1)} %bitcast.87, bf16[2048,128]{1,0:T(8,128)(2,1)} %bitcast.84, bf16[2048,128]{1,0:T(8,128)(2,1)} %bitcast.86, f32[2048,16]{1,0:T(8,128)} %get-tuple-element.27.dec_ref, ...), custom_call_target="tpu_custom_call" | custom-call | tf_op jit(solution)/shard_map/pallas_call | solution.py:74
  93.9 19.5 %reshape.40 = f32[16,4,8,64,4]{4,3,2,1,0:T(8,128)} reshape(f32[64,2048]{1,0:T(8,128)} %get-tuple-element.9) | data formatting | bytes 1048576 | tf_op jit(solution)/shard_map/reshape | solution.py:117
  113.4 16.0 %copy.57 = f32[16,4,8,64,4]{0,2,4,1,3:T(8,128)} copy(f32[16,4,8,64,4]{4,3,2,1,0:T(8,128)} %reshape.40) | data formatting | bytes 1048576 | tf_op jit(solution)/shard_map/reshape | solution.py:117
  129.4 4.2 %reshape.48 = f32[64,1,2048]{2,1,0:T(1,128)} reshape(f32[64,4,4,8,16]{4,3,2,1,0:T(8,128)} %bitcast.77) | data formatting | bytes 1048576
  133.6 6.4 %all-to-all-start.2 = ((f32[64,1,2048]{2,1,0:T(1,128)}), f32[64,1,2048]{2,1,0:T(1,128)S(1)}, u32[]{:S(2)}, u32[]{:S(2)}) async-start(f32[64,1,2048]{2,1,0:T(1,128)} %reshape.48), calls=%async_computation.2 | async-start | bytes 1048576 | tf_op jit(solution)/shard_map/all_to_all | solution.py:116
  140.0 0.8 exponential_bitcast_fusion
  140.9 16.2 %all-to-all-done.2 = f32[64,1,2048]{2,1,0:T(1,128)S(1)} async-done(((f32[64,1,2048]{2,1,0:T(1,128)}), f32[64,1,2048]{2,1,0:T(1,128)S(1)}, u32[]{:S(2)}, u32[]{:S(2)}) %all-to-all-start.2) | async-done | bytes 524320 | tf_op jit(solution)/shard_map/all_to_all | solution.py:116
  157.0 1.9 reduce.2
  158.9 2.8 %reshape.49 = f32[64,4,4,8,16]{4,3,2,1,0:T(8,128)} reshape(f32[64,2048]{1,0:T(8,128)S(1)} %reduce.2) | data formatting | bytes 1048576
  161.7 1.7 slice_bitcast_fusion.3
  167.1 0.6 fusion.6
  167.7 0.6 copy.69
  168.3 5.5 %all-to-all-start.4 = ((f32[8,4,16]{2,1,0:T(4,128)}), f32[8,4,16]{2,1,0:T(4,128)S(1)}, u32[]{:S(2)}, u32[]{:S(2)}) async-start(f32[8,4,16]{2,1,0:T(4,128)} %copy.69), calls=%async_computation.4 | async-start | bytes 32768 | tf_op jit(solution)/shard_map/all_to_all | solution.py:153
  173.8 1.3 fusion.13
  175.2 2.5 %reshape.50 = f32[64,1,1024]{2,1,0:T(1,128)} reshape(f32[64,4,8,32]{3,2,1,0:T(8,128)} %fusion.13) | data formatting | bytes 524288
  177.6 8.1 %all-to-all-done.4 = f32[8,4,16]{2,1,0:T(4,128)S(1)} async-done(((f32[8,4,16]{2,1,0:T(4,128)}), f32[8,4,16]{2,1,0:T(4,128)S(1)}, u32[]{:S(2)}, u32[]{:S(2)}) %all-to-all-start.4) | async-done | bytes 2080 | tf_op jit(solution)/shard_map/all_to_all | solution.py:153
  185.7 4.9 %all-to-all-start.3 = ((f32[64,1,1024]{2,1,0:T(1,128)}), f32[64,1,1024]{2,1,0:T(1,128)S(1)}, u32[]{:S(2)}, u32[]{:S(2)}) async-start(f32[64,1,1024]{2,1,0:T(1,128)} %reshape.50), calls=%async_computation.3 | async-start | bytes 524288 | tf_op jit(solution)/shard_map/all_to_all | solution.py:148
  190.7 0.6 multiply_multiply_fusion
  191.3 10.0 %all-to-all-done.3 = f32[64,1,1024]{2,1,0:T(1,128)S(1)} async-done(((f32[64,1,1024]{2,1,0:T(1,128)}), f32[64,1,1024]{2,1,0:T(1,128)S(1)}, u32[]{:S(2)}, u32[]{:S(2)}) %all-to-all-start.3) | async-done | bytes 262176 | tf_op jit(solution)/shard_map/all_to_all | solution.py:148
  201.3 1.3 reduce.3
  204.1 15.6 %multiply_reduce_fusion = (f32[2048,128]{1,0:T(8,128)S(1)}, f32[2048,128]{1,0:T(8,128)S(1)}) fusion(f32[128]{0:T(128)S(1)} %subtract_multiply_fusion, f32[2048,16]{1,0:T(8,128)S(1)} %get-tuple-element.22, f32[2048,16]{1,0:T(8,128)} %get-tuple-element.25, f32[128]{0:T(128)S(1)} %add_multiply_fusion, f32[2048,16]{1,0:T(8,128)S(1)} %get-tuple-element.21), kind=kLoop, calls=%fused_computation | loop fusion | flops 24641536 | bytes 2491392 | tf_op jit(solution)/shard_map/reduce_sum | solution.py:159
  219.7 1.4 fusion.1
  221.1 0.9 fusion
  222.0 0.9 fusion.2
  (57 shorter events, 6.2 us)
Async XLA Ops:
  133.6 23.4 %all-to-all-start.2 = ((f32[64,1,2048]{2,1,0:T(1,128)}), f32[64,1,2048]{2,1,0:T(1,128)S(1)}, u32[]{:S(2)}, u32[]{:S(2)}) async-start(f32[64,1,2048]{2,1,0:T(1,128)} %reshape.48), calls=%async_computation.2 | async-start | bytes 1048576 | tf_op jit(solution)/shard_map/all_to_all | solution.py:116
  164.9 2.2 copy-start
  165.6 25.1 %copy-start.8 = (f32[4,16]{1,0:T(4,128)S(1)}, f32[4,16]{1,0:T(4,128)}, u32[]{:S(2)}) copy-start(f32[4,16]{1,0:T(4,128)} %param.11) | copy-start | bytes 772
  166.2 37.6 %copy-start.1 = (f32[2048,16]{1,0:T(8,128)S(1)}, f32[2048,16]{1,0:T(8,128)}, u32[]{:S(2)}) copy-start(f32[2048,16]{1,0:T(8,128)} %get-tuple-element.26.w_ref) | copy-start | bytes 393220
  168.3 17.4 %all-to-all-start.4 = ((f32[8,4,16]{2,1,0:T(4,128)}), f32[8,4,16]{2,1,0:T(4,128)S(1)}, u32[]{:S(2)}, u32[]{:S(2)}) async-start(f32[8,4,16]{2,1,0:T(4,128)} %copy.69), calls=%async_computation.4 | async-start | bytes 32768 | tf_op jit(solution)/shard_map/all_to_all | solution.py:153
  175.2 44.5 %copy-start.2 = (bf16[1,2048,128]{2,1,0:T(8,128)(2,1)S(1)}, bf16[1,2048,128]{2,1,0:T(8,128)(2,1)}, u32[]{:S(2)}) copy-start(bf16[1,2048,128]{2,1,0:T(8,128)(2,1)} %param.9) | copy-start | bytes 1572868
  175.2 44.5 %copy-start.3 = (bf16[1,2048,128]{2,1,0:T(8,128)(2,1)S(1)}, bf16[1,2048,128]{2,1,0:T(8,128)(2,1)}, u32[]{:S(2)}) copy-start(bf16[1,2048,128]{2,1,0:T(8,128)(2,1)} %param.7) | copy-start | bytes 1572868
  185.7 15.5 %all-to-all-start.3 = ((f32[64,1,1024]{2,1,0:T(1,128)}), f32[64,1,1024]{2,1,0:T(1,128)S(1)}, u32[]{:S(2)}, u32[]{:S(2)}) async-start(f32[64,1,1024]{2,1,0:T(1,128)} %reshape.50), calls=%async_computation.3 | async-start | bytes 524288 | tf_op jit(solution)/shard_map/all_to_all | solution.py:148
  202.9 16.8 %copy-start.6 = (f32[2048,128]{1,0:T(8,128)S(1)}, f32[2048,128]{1,0:T(8,128)}, u32[]{:S(2)}) copy-start(f32[2048,128]{1,0:T(8,128)} %get-tuple-element.8) | copy-start | bytes 3145732
  202.9 16.8 %copy-start.7 = (f32[2048,128]{1,0:T(8,128)S(1)}, f32[2048,128]{1,0:T(8,128)}, u32[]{:S(2)}) copy-start(f32[2048,128]{1,0:T(8,128)} %get-tuple-element.10) | copy-start | bytes 3145732
  203.3 17.8 %copy-start.4 = (bf16[1,2048,128]{2,1,0:T(8,128)(2,1)S(1)}, bf16[1,2048,128]{2,1,0:T(8,128)(2,1)}, u32[]{:S(2)}) copy-start(bf16[1,2048,128]{2,1,0:T(8,128)(2,1)} %param.6) | copy-start | bytes 1572868
  203.3 18.8 %copy-start.5 = (bf16[1,2048,128]{2,1,0:T(8,128)(2,1)S(1)}, bf16[1,2048,128]{2,1,0:T(8,128)(2,1)}, u32[]{:S(2)}) copy-start(bf16[1,2048,128]{2,1,0:T(8,128)(2,1)} %param.8) | copy-start | bytes 1572868

commit v5 on v2

--- a/solution.py
+++ b/solution.py
@@ -65,7 +65,7 @@
     back_ref[...] = back
 
 
-def chunk_pass(keys, values, cotangent, queries, dec, weight, length, rows=256):
+def chunk_pass(keys, values, cotangent, queries, dec, weight, length, rows=128):
     channels, chunk = keys.shape
     order = dec.shape[1]
     rows = min(rows, channels)

time: 193 us -> 205 us (1.062)
  Pallas kernels: 38.2 us -> 49.6 us
    pallas_call x1, Pallas kernels: 38.2 us -> 49.6 us  [chunk_pass(): pl.pallas_call(functools.partial(chunk_kernel, length=length), grid=(chan...]
where the time goes in v5:
time: 205 us; the launch traced here: 204 us
  Pallas kernels  49.6 us (24%)
  blocking collectives  47.9 us (23%)
  other arithmetic  36 us (18%)
  waiting for transfers between devices  34 us (17%)
  local copies, waits for them, and re-layouts  18.4 us (9%)
  starting transfers between devices  16.7 us (8%)
    pallas_call x1, Pallas kernels, chunk_pass(): pl.pallas_call(functools.partial(chunk_kernel, length=length), grid=(chan...  49.6 us
    all_to_all x1, blocking collectives, body(): lax.all_to_all(jnp.broadcast_to(own[None], (n_dp,) + own.shape), 'dp', 0,...  28.2 us
    all_to_all x1, blocking collectives, body(): lax.all_to_all(jnp.broadcast_to(part, (n_dp, n_ctx, block, 2 * order)), '...  19.7 us
    all_to_all x1, waiting for transfers between devices, body(): stats = lax.all_to_all(stats, 'ctx', 1, 1, tiled=True)  16 us
    reduce_sum x1, other arithmetic, body(): jnp.sum((weight * carry_bwd)[:, :, None] * lead_bwd, axis=1)  14.5 us
    all_to_all x1, waiting for transfers between devices, body(): lax.all_to_all(jnp.concatenate([carry_fwd, carry_bwd], axis=-1), 'ctx', 1...  10.2 us
    all_to_all x1, waiting for transfers between devices, body(): total = jnp.sum(lax.all_to_all(cross_grp, 'dp', 0, 0, tiled=True), axis=0)  7.73 us
    unnamed x27, local copies, waits for them, and re-layouts  7.31 us
  transfers between devices with their start and end apart: 3, of which 3 were waited for; matrix products, arithmetic and copies ran while one was open for 3% of the time, Pallas kernels for 0%

profile of v5, /device:TPU:1, one launch (start us, length us, event | category | flops | bytes accessed | tf_op | source)
XLA Modules:
  0.0 203.6 jit_solution(4974448597926433593)
XLA Ops:
  0.6 0.8 pad_maximum_fusion.1
  1.5 28.2 %all_to_all.25 = f32[8,1,128]{2,1,0:T(1,128)S(1)} all-to-all(f32[8,1,128]{2,1,0:T(1,128)S(1)} %reshape.45), channel_id=1, replica_groups=mesh['dp'=8,'ctx'=64] {'dp'}, dimensions={0} | all-to-all | bytes 8192 | tf_op jit(solution)/shard_map/all_to_all | solution.py:97
  31.9 19.7 %all_to_all.26 = f32[64,1,1024]{2,1,0:T(1,128)S(1)} all-to-all(f32[64,1,1024]{2,1,0:T(1,128)S(1)} %reshape.47), channel_id=1, replica_groups=mesh['dp'=8,'ctx'=64] {'ctx'}, dimensions={0} | all-to-all | bytes 524288 | tf_op jit(solution)/shard_map/all_to_all | solution.py:100
  51.5 1.3 reduce.1
  53.5 2.2 %slice_negate_fusion = (f32[2048,16]{1,0:T(8,128)}, f32[2048,16]{1,0:T(8,128)}, f32[2048,16]{1,0:T(8,128)}) fusion(f32[2048,32]{1,0:T(8,128)S(1)} %bitcast.41), kind=kLoop, calls=%fused_computation.46 | loop fusion | flops 131072 | bytes 655360 | tf_op jit(solution)/shard_map/neg | solution.py:113
  55.8 49.6 %shard_map.101 = (f32[2048,128]{1,0:T(8,128)}, f32[2048,128]{1,0:T(8,128)}, f32[64,2048]{1,0:T(8,128)}) custom-call(bf16[2048,128]{1,0:T(8,128)(2,1)} %bitcast.48, bf16[2048,128]{1,0:T(8,128)(2,1)} %bitcast.50, bf16[2048,128]{1,0:T(8,128)(2,1)} %bitcast.47, bf16[2048,128]{1,0:T(8,128)(2,1)} %bitcast.49, f32[2048,16]{1,0:T(8,128)} %get-tuple-element.23.dec_ref, ...), custom_call_target="tpu_custom_call" | custom-call | tf_op jit(solution)/shard_map/pallas_call | solution.py:74
  105.4 1.2 reshape.40
  106.6 3.1 %copy.22 = f32[16,4,2048]{0,1,2:T(4,128)} copy(f32[16,4,2048]{2,1,0:T(4,128)S(1)} %reshape.40) | data formatting | bytes 1048576 | tf_op jit(solution)/shard_map/reshape | solution.py:112
  109.7 3.9 %reshape_reshape.3 = f32[8,64,4,64]{3,2,1,0:T(4,128)S(1)} reshape(f32[2048,4,16]{2,1,0:T(4,128)} %bitcast.40) | data formatting | bytes 1048576 | tf_op jit(solution)/shard_map/reshape;reshape | solution.py:117
  113.9 1.8 reshape.49
  115.7 6.4 %all-to-all-start.2 = ((f32[64,1,2048]{2,1,0:T(1,128)}), f32[64,1,2048]{2,1,0:T(1,128)S(1)}, u32[]{:S(2)}, u32[]{:S(2)}) async-start(f32[64,1,2048]{2,1,0:T(1,128)} %reshape.49), calls=%async_computation.2 | async-start | bytes 1048576 | tf_op jit(solution)/shard_map/all_to_all | solution.py:118
  122.1 0.8 exponential_bitcast_fusion
  122.9 16.0 %all-to-all-done.2 = f32[64,1,2048]{2,1,0:T(1,128)S(1)} async-done(((f32[64,1,2048]{2,1,0:T(1,128)}), f32[64,1,2048]{2,1,0:T(1,128)S(1)}, u32[]{:S(2)}, u32[]{:S(2)}) %all-to-all-start.2) | async-done | bytes 524320 | tf_op jit(solution)/shard_map/all_to_all | solution.py:118
  138.9 1.9 reduce.2
  140.8 0.7 reshape.50
  142.7 1.0 multiply_add_fusion.11
  143.9 1.0 multiply_add_fusion.10
  145.1 1.0 multiply_add_fusion.9
  146.2 1.1 multiply_add_fusion.8
  147.4 0.9 multiply_add_fusion.7
  148.5 1.8 fusion.5
  150.3 5.6 %all-to-all-start.4 = ((f32[8,4,16]{2,1,0:T(4,128)}), f32[8,4,16]{2,1,0:T(4,128)S(1)}, u32[]{:S(2)}, u32[]{:S(2)}) async-start(f32[8,4,16]{2,1,0:T(4,128)} %get-tuple-element.13), calls=%async_computation.4 | async-start | bytes 32768 | tf_op jit(solution)/shard_map/all_to_all | solution.py:153
  155.9 1.6 fusion.11
  157.5 2.6 %reshape.51 = f32[64,1,1024]{2,1,0:T(1,128)} reshape(f32[64,8,4,32]{3,2,1,0:T(4,128)} %fusion.11) | data formatting | bytes 524288
  160.1 7.7 %all-to-all-done.4 = f32[8,4,16]{2,1,0:T(4,128)S(1)} async-done(((f32[8,4,16]{2,1,0:T(4,128)}), f32[8,4,16]{2,1,0:T(4,128)S(1)}, u32[]{:S(2)}, u32[]{:S(2)}) %all-to-all-start.4) | async-done | bytes 2080 | tf_op jit(solution)/shard_map/all_to_all | solution.py:153
  167.8 4.7 %all-to-all-start.3 = ((f32[64,1,1024]{2,1,0:T(1,128)}), f32[64,1,1024]{2,1,0:T(1,128)S(1)}, u32[]{:S(2)}, u32[]{:S(2)}) async-start(f32[64,1,1024]{2,1,0:T(1,128)} %reshape.51), calls=%async_computation.3 | async-start | bytes 524288 | tf_op jit(solution)/shard_map/all_to_all | solution.py:148
  173.1 10.2 %all-to-all-done.3 = f32[64,1,1024]{2,1,0:T(1,128)S(1)} async-done(((f32[64,1,1024]{2,1,0:T(1,128)}), f32[64,1,1024]{2,1,0:T(1,128)S(1)}, u32[]{:S(2)}, u32[]{:S(2)}) %all-to-all-start.3) | async-done | bytes 262176 | tf_op jit(solution)/shard_map/all_to_all | solution.py:148
  183.3 1.3 reduce.3
  185.8 14.5 %multiply_reduce_fusion = (f32[2048,128]{1,0:T(8,128)S(1)}, f32[2048,128]{1,0:T(8,128)S(1)}) fusion(f32[128]{0:T(128)S(1)} %subtract_multiply_fusion, f32[2048,16]{1,0:T(8,128)S(1)} %get-tuple-element.20, f32[2048,16]{1,0:T(8,128)S(1)} %copy-done.7, f32[128]{0:T(128)S(1)} %add_multiply_fusion, f32[2048,16]{1,0:T(8,128)S(1)} %get-tuple-element.19), kind=kLoop, calls=%fused_computation | loop fusion | flops 24641536 | bytes 2491392 | tf_op jit(solution)/shard_map/reduce_sum | solution.py:159
  200.4 1.3 fusion.1
  201.7 0.9 fusion
  202.7 0.9 fusion.2
  (48 shorter events, 6.8 us)
Async XLA Ops:
  115.7 23.3 %all-to-all-start.2 = ((f32[64,1,2048]{2,1,0:T(1,128)}), f32[64,1,2048]{2,1,0:T(1,128)S(1)}, u32[]{:S(2)}, u32[]{:S(2)}) async-start(f32[64,1,2048]{2,1,0:T(1,128)} %reshape.49), calls=%async_computation.2 | async-start | bytes 1048576 | tf_op jit(solution)/shard_map/all_to_all | solution.py:118
  150.3 22.2 %copy-start.8 = (f32[4,16]{1,0:T(4,128)S(1)}, f32[4,16]{1,0:T(4,128)}, u32[]{:S(2)}) copy-start(f32[4,16]{1,0:T(4,128)} %param.11) | copy-start | bytes 772
  150.3 17.5 %all-to-all-start.4 = ((f32[8,4,16]{2,1,0:T(4,128)}), f32[8,4,16]{2,1,0:T(4,128)S(1)}, u32[]{:S(2)}, u32[]{:S(2)}) async-start(f32[8,4,16]{2,1,0:T(4,128)} %get-tuple-element.13), calls=%async_computation.4 | async-start | bytes 32768 | tf_op jit(solution)/shard_map/all_to_all | solution.py:153
  155.9 29.4 %copy-start = (f32[2048,16]{1,0:T(8,128)S(1)}, f32[2048,16]{1,0:T(8,128)}, u32[]{:S(2)}) copy-start(f32[2048,16]{1,0:T(8,128)} %get-tuple-element.22.w_ref) | copy-start | bytes 393220
  167.8 15.5 %all-to-all-start.3 = ((f32[64,1,1024]{2,1,0:T(1,128)}), f32[64,1,1024]{2,1,0:T(1,128)S(1)}, u32[]{:S(2)}, u32[]{:S(2)}) async-start(f32[64,1,1024]{2,1,0:T(1,128)} %reshape.51), calls=%async_computation.3 | async-start | bytes 524288 | tf_op jit(solution)/shard_map/all_to_all | solution.py:148
  184.6 1.2 copy-start.7
  185.8 14.5 %copy-start.1 = (bf16[1,2048,128]{2,1,0:T(8,128)(2,1)S(1)}, bf16[1,2048,128]{2,1,0:T(8,128)(2,1)}, u32[]{:S(2)}) copy-start(bf16[1,2048,128]{2,1,0:T(8,128)(2,1)} %param.9) | copy-start | bytes 1572868
  185.8 14.6 %copy-start.2 = (bf16[1,2048,128]{2,1,0:T(8,128)(2,1)S(1)}, bf16[1,2048,128]{2,1,0:T(8,128)(2,1)}, u32[]{:S(2)}) copy-start(bf16[1,2048,128]{2,1,0:T(8,128)(2,1)} %param.7) | copy-start | bytes 1572868
  185.8 14.6 %copy-start.5 = (f32[2048,128]{1,0:T(8,128)S(1)}, f32[2048,128]{1,0:T(8,128)}, u32[]{:S(2)}) copy-start(f32[2048,128]{1,0:T(8,128)} %get-tuple-element.8) | copy-start | bytes 3145732
  185.8 14.6 %copy-start.6 = (f32[2048,128]{1,0:T(8,128)S(1)}, f32[2048,128]{1,0:T(8,128)}, u32[]{:S(2)}) copy-start(f32[2048,128]{1,0:T(8,128)} %get-tuple-element.10) | copy-start | bytes 3145732
  200.4 1.4 copy-start.3
  200.4 2.3 %copy-start.4 = (bf16[1,2048,128]{2,1,0:T(8,128)(2,1)S(1)}, bf16[1,2048,128]{2,1,0:T(8,128)(2,1)}, u32[]{:S(2)}) copy-start(bf16[1,2048,128]{2,1,0:T(8,128)(2,1)} %param.8) | copy-start | bytes 1572868

commit v6 on v5

--- a/solution.py
+++ b/solution.py
@@ -65,7 +65,7 @@
     back_ref[...] = back
 
 
-def chunk_pass(keys, values, cotangent, queries, dec, weight, length, rows=128):
+def chunk_pass(keys, values, cotangent, queries, dec, weight, length, rows=512):
     channels, chunk = keys.shape
     order = dec.shape[1]
     rows = min(rows, channels)

time: 205 us -> 194 us (0.946)
  Pallas kernels: 49.6 us -> 39 us
    pallas_call x1, Pallas kernels: 49.6 us -> 39 us  [chunk_pass(): pl.pallas_call(functools.partial(chunk_kernel, length=length), grid=(chan...]
where the time goes in v6:
time: 194 us; the launch traced here: 193 us
  blocking collectives  47.9 us (25%)
  Pallas kernels  39 us (20%)
  other arithmetic  36 us (19%)
  waiting for transfers between devices  34.2 us (18%)
  local copies, waits for them, and re-layouts  18.4 us (9%)
  starting transfers between devices  16.6 us (9%)
    pallas_call x1, Pallas kernels, chunk_pass(): pl.pallas_call(functools.partial(chunk_kernel, length=length), grid=(chan...  39 us
    all_to_all x1, blocking collectives, body(): lax.all_to_all(jnp.broadcast_to(own[None], (n_dp,) + own.shape), 'dp', 0,...  28.2 us
    all_to_all x1, blocking collectives, body(): lax.all_to_all(jnp.broadcast_to(part, (n_dp, n_ctx, block, 2 * order)), '...  19.7 us
    all_to_all x1, waiting for transfers between devices, body(): stats = lax.all_to_all(stats, 'ctx', 1, 1, tiled=True)  16.2 us
    reduce_sum x1, other arithmetic, body(): jnp.sum((weight * carry_bwd)[:, :, None] * lead_bwd, axis=1)  14.5 us
    all_to_all x1, waiting for transfers between devices, body(): lax.all_to_all(jnp.concatenate([carry_fwd, carry_bwd], axis=-1), 'ctx', 1...  10.2 us
    all_to_all x1, waiting for transfers between devices, body(): total = jnp.sum(lax.all_to_all(cross_grp, 'dp', 0, 0, tiled=True), axis=0)  7.73 us
    unnamed x27, local copies, waits for them, and re-layouts  7.31 us
  transfers between devices with their start and end apart: 3, of which 3 were waited for; matrix products, arithmetic and copies ran while one was open for 3% of the time, Pallas kernels for 0%

profile of v6, /device:TPU:1, one launch (start us, length us, event | category | flops | bytes accessed | tf_op | source)
XLA Modules:
  0.0 193.0 jit_solution(18017160944513632797)
XLA Ops:
  0.6 0.8 pad_maximum_fusion.1
  1.5 28.2 %all_to_all.25 = f32[8,1,128]{2,1,0:T(1,128)S(1)} all-to-all(f32[8,1,128]{2,1,0:T(1,128)S(1)} %reshape.45), channel_id=1, replica_groups=mesh['dp'=8,'ctx'=64] {'dp'}, dimensions={0} | all-to-all | bytes 8192 | tf_op jit(solution)/shard_map/all_to_all | solution.py:97
  31.9 19.7 %all_to_all.26 = f32[64,1,1024]{2,1,0:T(1,128)S(1)} all-to-all(f32[64,1,1024]{2,1,0:T(1,128)S(1)} %reshape.47), channel_id=1, replica_groups=mesh['dp'=8,'ctx'=64] {'ctx'}, dimensions={0} | all-to-all | bytes 524288 | tf_op jit(solution)/shard_map/all_to_all | solution.py:100
  51.5 1.3 reduce.1
  53.5 2.2 %slice_negate_fusion = (f32[2048,16]{1,0:T(8,128)}, f32[2048,16]{1,0:T(8,128)}, f32[2048,16]{1,0:T(8,128)}) fusion(f32[2048,32]{1,0:T(8,128)S(1)} %bitcast.41), kind=kLoop, calls=%fused_computation.46 | loop fusion | flops 131072 | bytes 655360 | tf_op jit(solution)/shard_map/neg | solution.py:113
  55.8 39.0 %shard_map.101 = (f32[2048,128]{1,0:T(8,128)}, f32[2048,128]{1,0:T(8,128)}, f32[64,2048]{1,0:T(8,128)}) custom-call(bf16[2048,128]{1,0:T(8,128)(2,1)} %bitcast.48, bf16[2048,128]{1,0:T(8,128)(2,1)} %bitcast.50, bf16[2048,128]{1,0:T(8,128)(2,1)} %bitcast.47, bf16[2048,128]{1,0:T(8,128)(2,1)} %bitcast.49, f32[2048,16]{1,0:T(8,128)} %get-tuple-element.23.dec_ref, ...), custom_call_target="tpu_custom_call" | custom-call | tf_op jit(solution)/shard_map/pallas_call | solution.py:74
  94.8 1.2 reshape.40
  96.0 3.1 %copy.22 = f32[16,4,2048]{0,1,2:T(4,128)} copy(f32[16,4,2048]{2,1,0:T(4,128)S(1)} %reshape.40) | data formatting | bytes 1048576 | tf_op jit(solution)/shard_map/reshape | solution.py:112
  99.1 3.9 %reshape_reshape.3 = f32[8,64,4,64]{3,2,1,0:T(4,128)S(1)} reshape(f32[2048,4,16]{2,1,0:T(4,128)} %bitcast.40) | data formatting | bytes 1048576 | tf_op jit(solution)/shard_map/reshape;reshape | solution.py:117
  103.3 1.8 reshape.49
  105.1 6.3 %all-to-all-start.2 = ((f32[64,1,2048]{2,1,0:T(1,128)}), f32[64,1,2048]{2,1,0:T(1,128)S(1)}, u32[]{:S(2)}, u32[]{:S(2)}) async-start(f32[64,1,2048]{2,1,0:T(1,128)} %reshape.49), calls=%async_computation.2 | async-start | bytes 1048576 | tf_op jit(solution)/shard_map/all_to_all | solution.py:118
  111.3 0.8 exponential_bitcast_fusion
  112.1 16.2 %all-to-all-done.2 = f32[64,1,2048]{2,1,0:T(1,128)S(1)} async-done(((f32[64,1,2048]{2,1,0:T(1,128)}), f32[64,1,2048]{2,1,0:T(1,128)S(1)}, u32[]{:S(2)}, u32[]{:S(2)}) %all-to-all-start.2) | async-done | bytes 524320 | tf_op jit(solution)/shard_map/all_to_all | solution.py:118
  128.3 1.9 reduce.2
  130.2 0.7 reshape.50
  132.1 1.0 multiply_add_fusion.11
  133.3 1.0 multiply_add_fusion.10
  134.5 1.0 multiply_add_fusion.9
  135.6 1.1 multiply_add_fusion.8
  136.8 0.9 multiply_add_fusion.7
  137.8 1.8 fusion.5
  139.7 5.6 %all-to-all-start.4 = ((f32[8,4,16]{2,1,0:T(4,128)}), f32[8,4,16]{2,1,0:T(4,128)S(1)}, u32[]{:S(2)}, u32[]{:S(2)}) async-start(f32[8,4,16]{2,1,0:T(4,128)} %get-tuple-element.13), calls=%async_computation.4 | async-start | bytes 32768 | tf_op jit(solution)/shard_map/all_to_all | solution.py:153
  145.3 1.6 fusion.11
  146.9 2.6 %reshape.51 = f32[64,1,1024]{2,1,0:T(1,128)} reshape(f32[64,8,4,32]{3,2,1,0:T(4,128)} %fusion.11) | data formatting | bytes 524288
  149.5 7.7 %all-to-all-done.4 = f32[8,4,16]{2,1,0:T(4,128)S(1)} async-done(((f32[8,4,16]{2,1,0:T(4,128)}), f32[8,4,16]{2,1,0:T(4,128)S(1)}, u32[]{:S(2)}, u32[]{:S(2)}) %all-to-all-start.4) | async-done | bytes 2080 | tf_op jit(solution)/shard_map/all_to_all | solution.py:153
  157.2 4.7 %all-to-all-start.3 = ((f32[64,1,1024]{2,1,0:T(1,128)}), f32[64,1,1024]{2,1,0:T(1,128)S(1)}, u32[]{:S(2)}, u32[]{:S(2)}) async-start(f32[64,1,1024]{2,1,0:T(1,128)} %reshape.51), calls=%async_computation.3 | async-start | bytes 524288 | tf_op jit(solution)/shard_map/all_to_all | solution.py:148
  162.5 10.2 %all-to-all-done.3 = f32[64,1,1024]{2,1,0:T(1,128)S(1)} async-done(((f32[64,1,1024]{2,1,0:T(1,128)}), f32[64,1,1024]{2,1,0:T(1,128)S(1)}, u32[]{:S(2)}, u32[]{:S(2)}) %all-to-all-start.3) | async-done | bytes 262176 | tf_op jit(solution)/shard_map/all_to_all | solution.py:148
  172.7 1.3 reduce.3
  175.2 14.5 %multiply_reduce_fusion = (f32[2048,128]{1,0:T(8,128)S(1)}, f32[2048,128]{1,0:T(8,128)S(1)}) fusion(f32[128]{0:T(128)S(1)} %subtract_multiply_fusion, f32[2048,16]{1,0:T(8,128)S(1)} %get-tuple-element.20, f32[2048,16]{1,0:T(8,128)S(1)} %copy-done.7, f32[128]{0:T(128)S(1)} %add_multiply_fusion, f32[2048,16]{1,0:T(8,128)S(1)} %get-tuple-element.19), kind=kLoop, calls=%fused_computation | loop fusion | flops 24641536 | bytes 2491392 | tf_op jit(solution)/shard_map/reduce_sum | solution.py:159
  189.8 1.3 fusion.1
  191.1 0.9 fusion
  192.1 0.9 fusion.2
  (48 shorter events, 6.8 us)
Async XLA Ops:
  105.1 23.3 %all-to-all-start.2 = ((f32[64,1,2048]{2,1,0:T(1,128)}), f32[64,1,2048]{2,1,0:T(1,128)S(1)}, u32[]{:S(2)}, u32[]{:S(2)}) async-start(f32[64,1,2048]{2,1,0:T(1,128)} %reshape.49), calls=%async_computation.2 | async-start | bytes 1048576 | tf_op jit(solution)/shard_map/all_to_all | solution.py:118
  139.7 22.2 %copy-start.8 = (f32[4,16]{1,0:T(4,128)S(1)}, f32[4,16]{1,0:T(4,128)}, u32[]{:S(2)}) copy-start(f32[4,16]{1,0:T(4,128)} %param.11) | copy-start | bytes 772
  139.7 17.5 %all-to-all-start.4 = ((f32[8,4,16]{2,1,0:T(4,128)}), f32[8,4,16]{2,1,0:T(4,128)S(1)}, u32[]{:S(2)}, u32[]{:S(2)}) async-start(f32[8,4,16]{2,1,0:T(4,128)} %get-tuple-element.13), calls=%async_computation.4 | async-start | bytes 32768 | tf_op jit(solution)/shard_map/all_to_all | solution.py:153
  145.3 29.4 %copy-start = (f32[2048,16]{1,0:T(8,128)S(1)}, f32[2048,16]{1,0:T(8,128)}, u32[]{:S(2)}) copy-start(f32[2048,16]{1,0:T(8,128)} %get-tuple-element.22.w_ref) | copy-start | bytes 393220
  157.2 15.5 %all-to-all-start.3 = ((f32[64,1,1024]{2,1,0:T(1,128)}), f32[64,1,1024]{2,1,0:T(1,128)S(1)}, u32[]{:S(2)}, u32[]{:S(2)}) async-start(f32[64,1,1024]{2,1,0:T(1,128)} %reshape.51), calls=%async_computation.3 | async-start | bytes 524288 | tf_op jit(solution)/shard_map/all_to_all | solution.py:148
  174.0 1.2 copy-start.7
  175.2 14.5 %copy-start.1 = (bf16[1,2048,128]{2,1,0:T(8,128)(2,1)S(1)}, bf16[1,2048,128]{2,1,0:T(8,128)(2,1)}, u32[]{:S(2)}) copy-start(bf16[1,2048,128]{2,1,0:T(8,128)(2,1)} %param.9) | copy-start | bytes 1572868
  175.2 14.6 %copy-start.2 = (bf16[1,2048,128]{2,1,0:T(8,128)(2,1)S(1)}, bf16[1,2048,128]{2,1,0:T(8,128)(2,1)}, u32[]{:S(2)}) copy-start(bf16[1,2048,128]{2,1,0:T(8,128)(2,1)} %param.7) | copy-start | bytes 1572868
  175.2 14.6 %copy-start.5 = (f32[2048,128]{1,0:T(8,128)S(1)}, f32[2048,128]{1,0:T(8,128)}, u32[]{:S(2)}) copy-start(f32[2048,128]{1,0:T(8,128)} %get-tuple-element.8) | copy-start | bytes 3145732
  175.2 14.6 %copy-start.6 = (f32[2048,128]{1,0:T(8,128)S(1)}, f32[2048,128]{1,0:T(8,128)}, u32[]{:S(2)}) copy-start(f32[2048,128]{1,0:T(8,128)} %get-tuple-element.10) | copy-start | bytes 3145732
  189.8 1.4 copy-start.3
  189.8 2.3 %copy-start.4 = (bf16[1,2048,128]{2,1,0:T(8,128)(2,1)S(1)}, bf16[1,2048,128]{2,1,0:T(8,128)(2,1)}, u32[]{:S(2)}) copy-start(bf16[1,2048,128]{2,1,0:T(8,128)(2,1)} %param.8) | copy-start | bytes 1572868

commit v7 on v2

--- a/solution.py
+++ b/solution.py
@@ -111,7 +111,6 @@
     )
     stats = stats.reshape(order, 4, channels).transpose(2, 1, 0).reshape(channels, 4 * order)
     lead_fwd = jnp.exp(-dk * ((pos + 1) / length))
-    lead_bwd = jnp.exp(-dk * ((chunk - pos) / length))
 
     groups = channels // (n_dp * n_ctx)
     stats = stats.reshape(n_dp, n_ctx, groups, 4 * order)
@@ -156,7 +155,9 @@
     grad_residues = total * own_scale / math.sqrt(seq_count * n_dp * length)
 
     conv_full = conv_intra + jnp.sum((weight * carry_fwd)[:, :, None] * lead_fwd, axis=1)
-    back_full = back_intra + jnp.sum((weight * carry_bwd)[:, :, None] * lead_bwd, axis=1)
+    back_full = back_intra + jnp.flip(
+        jnp.sum((weight * carry_bwd)[:, :, None] * lead_fwd, axis=1), axis=1
+    )
     conv_f = conv_full.astype(jnp.bfloat16).astype(f32)[None]
     back_f = back_full.astype(jnp.bfloat16).astype(f32)[None]
     mixed = (queries.astype(f32) * conv_f).astype(jnp.bfloat16)

time: 193 us -> 204 us (1.057)
  local copies, waits for them, and re-layouts: 18.4 us -> 25.9 us
  other arithmetic: 36 us -> 38.9 us
    rev x0 -> x1, local copies, waits for them, and re-layouts: none -> 7.5 us  [body(): jnp.flip(jnp.sum((weight * carry_bwd)[:, :, None] * lead_fwd, axis=1), ax...]
    unnamed x27 -> x25, local copies, waits for them, and re-layouts: 7.31 us -> 7.31 us
where the time goes in v7:
time: 204 us; the launch traced here: 202 us
  blocking collectives  47.9 us (23%)
  other arithmetic  38.9 us (19%)
  Pallas kernels  38.2 us (19%)
  waiting for transfers between devices  34.2 us (17%)
  local copies, waits for them, and re-layouts  25.9 us (13%)
  starting transfers between devices  16.6 us (8%)
    pallas_call x1, Pallas kernels, chunk_pass(): pl.pallas_call(functools.partial(chunk_kernel, length=length), grid=(chan...  38.2 us
    all_to_all x1, blocking collectives, body(): lax.all_to_all(jnp.broadcast_to(own[None], (n_dp,) + own.shape), 'dp', 0,...  28.2 us
    all_to_all x1, blocking collectives, body(): lax.all_to_all(jnp.broadcast_to(part, (n_dp, n_ctx, block, 2 * order)), '...  19.7 us
    all_to_all x1, waiting for transfers between devices, body(): stats = lax.all_to_all(stats, 'ctx', 1, 1, tiled=True)  16.2 us
    reduce_sum x1, other arithmetic, body(): jnp.sum((weight * carry_bwd)[:, :, None] * lead_fwd, axis=1)  15.9 us
    all_to_all x1, waiting for transfers between devices, body(): lax.all_to_all(jnp.concatenate([carry_fwd, carry_bwd], axis=-1), 'ctx', 1...  10.2 us
    all_to_all x1, waiting for transfers between devices, body(): total = jnp.sum(lax.all_to_all(cross_grp, 'dp', 0, 0, tiled=True), axis=0)  7.72 us
    rev x1, local copies, waits for them, and re-layouts, body(): jnp.flip(jnp.sum((weight * carry_bwd)[:, :, None] * lead_fwd, axis=1), ax...  7.5 us
  transfers between devices with their start and end apart: 3, of which 3 were waited for; matrix products, arithmetic and copies ran while one was open for 3% of the time, Pallas kernels for 0%

profile of v7, /device:TPU:1, one launch (start us, length us, event | category | flops | bytes accessed | tf_op | source)
XLA Modules:
  0.0 202.5 jit_solution(9712685610211197261)
XLA Ops:
  0.6 0.8 pad_maximum_fusion.1
  1.5 28.2 %all_to_all.25 = f32[8,1,128]{2,1,0:T(1,128)S(1)} all-to-all(f32[8,1,128]{2,1,0:T(1,128)S(1)} %reshape.40), channel_id=1, replica_groups=mesh['dp'=8,'ctx'=64] {'dp'}, dimensions={0} | all-to-all | bytes 8192 | tf_op jit(solution)/shard_map/all_to_all | solution.py:97
  31.9 19.7 %all_to_all.26 = f32[64,1,1024]{2,1,0:T(1,128)S(1)} all-to-all(f32[64,1,1024]{2,1,0:T(1,128)S(1)} %reshape.42), channel_id=1, replica_groups=mesh['dp'=8,'ctx'=64] {'ctx'}, dimensions={0} | all-to-all | bytes 524288 | tf_op jit(solution)/shard_map/all_to_all | solution.py:100
  51.5 1.3 reduce.1
  53.5 2.1 %slice_negate_fusion = (f32[2048,16]{1,0:T(8,128)}, f32[2048,16]{1,0:T(8,128)}, f32[2048,16]{1,0:T(8,128)}) fusion(f32[2048,32]{1,0:T(8,128)S(1)} %bitcast.41), kind=kLoop, calls=%fused_computation.46 | loop fusion | flops 131072 | bytes 655360 | tf_op jit(solution)/shard_map/neg | solution.py:113
  55.7 38.2 %shard_map.101 = (f32[2048,128]{1,0:T(8,128)}, f32[2048,128]{1,0:T(8,128)}, f32[64,2048]{1,0:T(8,128)}) custom-call(bf16[2048,128]{1,0:T(8,128)(2,1)} %bitcast.48, bf16[2048,128]{1,0:T(8,128)(2,1)} %bitcast.50, bf16[2048,128]{1,0:T(8,128)(2,1)} %bitcast.47, bf16[2048,128]{1,0:T(8,128)(2,1)} %bitcast.49, f32[2048,16]{1,0:T(8,128)} %get-tuple-element.23.dec_ref, ...), custom_call_target="tpu_custom_call" | custom-call | tf_op jit(solution)/shard_map/pallas_call | solution.py:74
  93.9 1.2 reshape.35
  95.0 3.1 %copy.22 = f32[16,4,2048]{0,1,2:T(4,128)} copy(f32[16,4,2048]{2,1,0:T(4,128)S(1)} %reshape.35) | data formatting | bytes 1048576 | tf_op jit(solution)/shard_map/reshape | solution.py:112
  98.1 3.9 %reshape_reshape.3 = f32[8,64,4,64]{3,2,1,0:T(4,128)S(1)} reshape(f32[2048,4,16]{2,1,0:T(4,128)} %bitcast.40) | data formatting | bytes 1048576 | tf_op jit(solution)/shard_map/reshape;reshape | solution.py:116
  102.3 1.8 reshape.44
  104.1 6.3 %all-to-all-start.2 = ((f32[64,1,2048]{2,1,0:T(1,128)}), f32[64,1,2048]{2,1,0:T(1,128)S(1)}, u32[]{:S(2)}, u32[]{:S(2)}) async-start(f32[64,1,2048]{2,1,0:T(1,128)} %reshape.44), calls=%async_computation.2 | async-start | bytes 1048576 | tf_op jit(solution)/shard_map/all_to_all | solution.py:117
  110.4 0.8 exponential_bitcast_fusion
  111.2 16.2 %all-to-all-done.2 = f32[64,1,2048]{2,1,0:T(1,128)S(1)} async-done(((f32[64,1,2048]{2,1,0:T(1,128)}), f32[64,1,2048]{2,1,0:T(1,128)S(1)}, u32[]{:S(2)}, u32[]{:S(2)}) %all-to-all-start.2) | async-done | bytes 524320 | tf_op jit(solution)/shard_map/all_to_all | solution.py:117
  127.4 1.9 reduce.2
  131.1 1.0 multiply_add_fusion.11
  132.3 1.0 multiply_add_fusion.10
  133.5 1.0 multiply_add_fusion.9
  134.7 1.1 multiply_add_fusion.8
  135.9 0.9 multiply_add_fusion.7
  136.9 1.8 fusion.5
  138.7 5.6 %all-to-all-start.4 = ((f32[8,4,16]{2,1,0:T(4,128)}), f32[8,4,16]{2,1,0:T(4,128)S(1)}, u32[]{:S(2)}, u32[]{:S(2)}) async-start(f32[8,4,16]{2,1,0:T(4,128)} %get-tuple-element.13), calls=%async_computation.4 | async-start | bytes 32768 | tf_op jit(solution)/shard_map/all_to_all | solution.py:152
  144.3 1.6 fusion.11
  145.9 2.6 %reshape.46 = f32[64,1,1024]{2,1,0:T(1,128)} reshape(f32[64,8,4,32]{3,2,1,0:T(4,128)} %fusion.11) | data formatting | bytes 524288
  148.5 7.7 %all-to-all-done.4 = f32[8,4,16]{2,1,0:T(4,128)S(1)} async-done(((f32[8,4,16]{2,1,0:T(4,128)}), f32[8,4,16]{2,1,0:T(4,128)S(1)}, u32[]{:S(2)}, u32[]{:S(2)}) %all-to-all-start.4) | async-done | bytes 2080 | tf_op jit(solution)/shard_map/all_to_all | solution.py:152
  156.2 4.7 %all-to-all-start.3 = ((f32[64,1,1024]{2,1,0:T(1,128)}), f32[64,1,1024]{2,1,0:T(1,128)S(1)}, u32[]{:S(2)}, u32[]{:S(2)}) async-start(f32[64,1,1024]{2,1,0:T(1,128)} %reshape.46), calls=%async_computation.3 | async-start | bytes 524288 | tf_op jit(solution)/shard_map/all_to_all | solution.py:147
  161.5 10.2 %all-to-all-done.3 = f32[64,1,1024]{2,1,0:T(1,128)S(1)} async-done(((f32[64,1,1024]{2,1,0:T(1,128)}), f32[64,1,1024]{2,1,0:T(1,128)S(1)}, u32[]{:S(2)}, u32[]{:S(2)}) %all-to-all-start.3) | async-done | bytes 262176 | tf_op jit(solution)/shard_map/all_to_all | solution.py:147
  171.8 1.3 reduce.3
  174.3 15.9 %multiply_reduce_fusion = (f32[2048,128]{1,0:T(8,128)}, f32[2048,128]{1,0:T(8,128)}) fusion(f32[2048,16]{1,0:T(8,128)S(1)} %get-tuple-element.20, f32[128]{0:T(128)S(1)} %add_multiply_fusion, f32[2048,16]{1,0:T(8,128)S(1)} %copy-done.6, f32[2048,16]{1,0:T(8,128)S(1)} %get-tuple-element.19), kind=kLoop, calls=%fused_computation | loop fusion | flops 20447232 | bytes 2490880 | tf_op jit(solution)/shard_map/reduce_sum | solution.py:159
  190.2 7.5 %rev.4 = f32[2048,128]{1,0:T(8,128)S(1)} reverse(f32[2048,128]{1,0:T(8,128)} %get-tuple-element.11), dimensions={1} | reverse | bytes 2097152 | tf_op jit(solution)/shard_map/jit(_flip)/rev | solution.py:158
  197.7 2.9 %fusion.1 = (bf16[1,2048,128]{2,1,0:T(8,128)(2,1)}, bf16[1,2048,128]{2,1,0:T(8,128)(2,1)S(1)}, bf16[1,2048,128]{2,1,0:T(8,128)(2,1)}, bf16[1,2048,128]{2,1,0:T(8,128)(2,1)S(1)}) fusion(bf16[1,2048,128]{2,1,0:T(8,128)(2,1)S(1)} %copy-done.1, f32[2048,128]{1,0:T(8,128)S(1)} %copy-done.5, f32[2048,128]{1,0:T(8,128)} %get-tuple-element.12, ...), kind=kLoop, calls=%fused_computation.8 | loop fusion | flops 3145728 | bytes 7340032 | tf_op jit(solution)/shard_map/convert_element_type | solution.py:164
  200.6 0.9 fusion
  201.6 0.9 fusion.2
  (46 shorter events, 7.5 us)
Async XLA Ops:
  104.1 23.3 %all-to-all-start.2 = ((f32[64,1,2048]{2,1,0:T(1,128)}), f32[64,1,2048]{2,1,0:T(1,128)S(1)}, u32[]{:S(2)}, u32[]{:S(2)}) async-start(f32[64,1,2048]{2,1,0:T(1,128)} %reshape.44), calls=%async_computation.2 | async-start | bytes 1048576 | tf_op jit(solution)/shard_map/all_to_all | solution.py:117
  138.7 22.2 %copy-start.7 = (f32[4,16]{1,0:T(4,128)S(1)}, f32[4,16]{1,0:T(4,128)}, u32[]{:S(2)}) copy-start(f32[4,16]{1,0:T(4,128)} %param.11) | copy-start | bytes 772
  138.7 17.5 %all-to-all-start.4 = ((f32[8,4,16]{2,1,0:T(4,128)}), f32[8,4,16]{2,1,0:T(4,128)S(1)}, u32[]{:S(2)}, u32[]{:S(2)}) async-start(f32[8,4,16]{2,1,0:T(4,128)} %get-tuple-element.13), calls=%async_computation.4 | async-start | bytes 32768 | tf_op jit(solution)/shard_map/all_to_all | solution.py:152
  144.3 29.4 %copy-start = (f32[2048,16]{1,0:T(8,128)S(1)}, f32[2048,16]{1,0:T(8,128)}, u32[]{:S(2)}) copy-start(f32[2048,16]{1,0:T(8,128)} %get-tuple-element.22.w_ref) | copy-start | bytes 393220
  156.2 15.5 %all-to-all-start.3 = ((f32[64,1,1024]{2,1,0:T(1,128)}), f32[64,1,1024]{2,1,0:T(1,128)S(1)}, u32[]{:S(2)}, u32[]{:S(2)}) async-start(f32[64,1,1024]{2,1,0:T(1,128)} %reshape.46), calls=%async_computation.3 | async-start | bytes 524288 | tf_op jit(solution)/shard_map/all_to_all | solution.py:147
  173.0 1.2 copy-start.6
  174.3 23.4 %copy-start.1 = (bf16[1,2048,128]{2,1,0:T(8,128)(2,1)S(1)}, bf16[1,2048,128]{2,1,0:T(8,128)(2,1)}, u32[]{:S(2)}) copy-start(bf16[1,2048,128]{2,1,0:T(8,128)(2,1)} %param.9) | copy-start | bytes 1572868
  174.3 23.4 %copy-start.2 = (bf16[1,2048,128]{2,1,0:T(8,128)(2,1)S(1)}, bf16[1,2048,128]{2,1,0:T(8,128)(2,1)}, u32[]{:S(2)}) copy-start(bf16[1,2048,128]{2,1,0:T(8,128)(2,1)} %param.7) | copy-start | bytes 1572868
  174.3 23.4 %copy-start.5 = (f32[2048,128]{1,0:T(8,128)S(1)}, f32[2048,128]{1,0:T(8,128)}, u32[]{:S(2)}) copy-start(f32[2048,128]{1,0:T(8,128)} %get-tuple-element.8) | copy-start | bytes 3145732
  197.6 3.0 %copy-start.3 = (bf16[1,2048,128]{2,1,0:T(8,128)(2,1)S(1)}, bf16[1,2048,128]{2,1,0:T(8,128)(2,1)}, u32[]{:S(2)}) copy-start(bf16[1,2048,128]{2,1,0:T(8,128)(2,1)} %param.6) | copy-start | bytes 1572868
  197.7 3.9 %copy-start.4 = (bf16[1,2048,128]{2,1,0:T(8,128)(2,1)S(1)}, bf16[1,2048,128]{2,1,0:T(8,128)(2,1)}, u32[]{:S(2)}) copy-start(bf16[1,2048,128]{2,1,0:T(8,128)(2,1)} %param.8) | copy-start | bytes 1572868
